TPU v7x, 256 devices: a whole 4x4x8 slice. The times are simulated.
256 devices in a mesh: env: 16 (over x, y_lo, core), pts: 16 (over y_hi, z).
Axes of the slice: x: 4, y: 4 (y_hi: 2, y_lo: 2; y = y_hi * 2 + y_lo), z: 8, core: 2. Of those that a mesh axis runs over, the one named last changes fastest.
Arguments:
- descriptors: float32 [1024, 16384], P('pts', 'env'), may hold values from -6 to 6
- env_weight: float32 [16384], P('env'), may hold values from 0.25 to 4
- points: float32 [2560, 1024], P('pts', 'env'), may hold values from -6 to 6
Outputs:
- panel_factor: float32 [2560, 512], P('env', 'pts')
- trailing: float32 [2048, 2048], P('env', 'pts')
All inputs are finite; a program needn't handle non-finite values.
Results may differ from a plain program's by a relative error of at most 0.0003.
Values sent between devices are 32-bit elements; how exact they have to be, the bound alone decides.
A program may use at most 64 MiB of HBM per device.

v0:
```python
import jax
import jax.numpy as jnp
from jax import lax
from jax.sharding import Mesh
from jax.sharding import PartitionSpec as P

PANEL = 512
PTS = ("pts_0", "pts_1")
ENV_PTS = ("env", "pts_0", "pts_1")


def joined_along(blocks, dim):
    lengths = list(blocks.shape[1:])
    lengths[dim] *= blocks.shape[0]
    return jnp.moveaxis(blocks, 0, dim).reshape(lengths)


def gather_in_order(shard, axes, order):
    blocks = shard[None]
    for k in order:
        blocks = lax.all_gather(blocks, axes[k], axis=0, tiled=True)
    held = [lax.axis_size(axes[k]) for k in reversed(order)]
    blocks = blocks.reshape(*held, *shard.shape)
    turned = sorted(range(len(order)), key=lambda place: order[len(order) - 1 - place])
    return blocks.transpose(*turned, *range(len(order), blocks.ndim)).reshape(-1, *shard.shape)


def gathered_by_axis(shard, axes, order, dim):
    return joined_along(gather_in_order(shard, axes, order), dim)


def cut_along(shard, dim, count):
    before, after = (shard.shape[:dim], shard.shape[dim + 1 :])
    return jnp.moveaxis(shard.reshape(*before, count, -1, *after), dim, 0)


def summed_on_arrival(shard, axis, dim):
    count = lax.axis_size(axis)
    blocks = lax.all_to_all(cut_along(shard, dim, count), axis, 0, 0, tiled=True)
    return jnp.sum(blocks, axis=0)


def cubed_kernel(features, targets):
    dots = lax.dot_general(
        features,
        targets,
        (((0,), (1,)), ((), ())),
        precision=lax.Precision.HIGHEST,
        preferred_element_type=jnp.float32,
    )
    scaled = dots / jnp.sqrt(jnp.float32(features.shape[0]))
    return 0.25 * scaled * scaled * scaled


def local_points(count, device, devices, block_size):
    positions = jnp.arange(count, dtype=jnp.int32)
    return block_size * (devices * (positions // block_size) + device) + positions % block_size


def local(descriptors, env_weight, points):
    env_count = lax.axis_size("env")
    pts_count = lax.axis_size(PTS)
    env_rank = lax.axis_index("env")
    pts_rank = lax.axis_index(PTS)
    features = gathered_by_axis(descriptors, PTS, (0, 1), 0)
    own_points = lax.all_gather(points, "env", axis=1, tiled=True)
    cols_dev = own_points.shape[0]
    total_points = cols_dev * pts_count
    rows_dev = total_points // env_count
    row_block = PANEL // env_count
    col_block = PANEL // pts_count
    cycles = total_points // PANEL
    own_tile = cubed_kernel(features, own_points)
    weighted = own_tile * env_weight[:, None]
    partial_gram = lax.dot_general(
        lax.all_gather(own_tile, PTS, axis=1, tiled=True),
        weighted,
        (((0,), (0,)), ((), ())),
        precision=lax.Precision.HIGHEST,
        preferred_element_type=jnp.float32,
    )
    partial_gram = partial_gram / jnp.float32(descriptors.shape[1] * env_count)
    natural = (
        partial_gram.reshape(pts_count, cycles, col_block, cols_dev)
        .transpose(1, 0, 2, 3)
        .reshape(total_points, cols_dev)
    )
    by_rows = (
        natural.reshape(cycles, env_count, row_block, cols_dev)
        .transpose(1, 0, 2, 3)
        .reshape(total_points, cols_dev)
    )
    gram_block = summed_on_arrival(by_rows, "env", 0)
    row_ids = local_points(rows_dev, env_rank, env_count, row_block)
    col_ids = local_points(cols_dev, pts_rank, pts_count, col_block)
    gram_block = gram_block + (row_ids[:, None] == col_ids[None, :]).astype(jnp.float32)
    corner = lax.all_gather(gram_block[None, :row_block, :col_block], ENV_PTS, axis=0, tiled=True)
    leading = (
        corner.reshape(env_count, pts_count, row_block, col_block)
        .transpose(0, 2, 1, 3)
        .reshape(PANEL, PANEL)
    )
    low_factor = jnp.linalg.cholesky(leading)
    panel_rows = lax.all_gather(gram_block[:, :col_block], PTS, axis=1, tiled=True)
    row_factor = jax.scipy.linalg.solve_triangular(low_factor, panel_rows.T, lower=True).T
    panel_out = lax.dynamic_slice_in_dim(row_factor, pts_rank * col_block, col_block, 1)
    top_rows = lax.all_gather(gram_block[:row_block, :], "env", axis=0, tiled=True)
    side_factor = jax.scipy.linalg.solve_triangular(low_factor, top_rows, lower=True).T[col_block:]
    update = lax.dot_general(
        row_factor[row_block:],
        side_factor,
        (((1,), (1,)), ((), ())),
        precision=lax.Precision.HIGHEST,
        preferred_element_type=jnp.float32,
    )
    trailing = gram_block[row_block:, col_block:] - update
    return (panel_out, trailing)


def solution(mesh):
    finer = Mesh(mesh.devices.reshape(mesh.shape["env"], 2, 8), ("env", "pts_0", "pts_1"))
    placed = (P(PTS, "env"), P("env"), P(PTS, "env"))
    return jax.shard_map(
        local,
        mesh=finer,
        in_specs=placed,
        out_specs=(P("env", PTS), P("env", PTS)),
        check_vma=False,
    )
```

profile of v0, /device:TPU:1, one launch (start us, length us, event | category | flops | bytes accessed | tf_op | source)
XLA Modules:
  0.0 1176.6 jit_solution(17212474054290347223)
XLA Ops:
  7.2 12.0 %all-gather = f32[128,1024]{1,0:T(8,128)} all-gather(f32[64,1024]{1,0:T(8,128)} %param.5), channel_id=2, replica_groups=mesh['env'=16,'pts_0'=2,'pts_1'=8] {'pts_0'}, dimensions={0}, use_global_device_ids=true | all-gather | bytes 786432 | tf_op jit(solution)/shard_map/all_gather | solution.py:21
  19.3 23.6 %all_gather.23 = f32[160,1024]{0,1:T(8,128)S(1)} all-gather(f32[160,64]{0,1:T(8,128)} %param.7), channel_id=1, replica_groups=mesh['env'=16,'pts_0'=2,'pts_1'=8] {'env'}, dimensions={1}, use_global_device_ids=true | all-gather | bytes 696320 | tf_op jit(solution)/shard_map/all_gather | solution.py:66
  42.9 33.4 %all-gather.6.cloned.1.call-done = f32[16,64,1024]{2,1,0:T(8,128)} async-done(((f32[2,64,1024]{2,1,0:T(8,128)}), f32[16,64,1024]{2,1,0:T(8,128)}) %all-gather.6.cloned.1.call-update) | async-done | bytes 4194320 | tf_op jit(solution)/shard_map/all_gather | solution.py:21
  78.8 3.8 multiply_multiply_fusion
  82.7 154.6 %all-gather.8.cloned.1.call-done = f32[1024,2560]{0,1:T(8,128)} async-done(((f32[1024,160]{0,1:T(8,128)}), f32[1024,2560]{0,1:T(8,128)}) %all-gather.8.cloned.1.call-update) | async-done | bytes 10485776 | tf_op jit(solution)/shard_map/all_gather | solution.py:76
  237.2 13.9 %convolution_multiply_fusion = f32[2560,160]{0,1:T(8,128)S(1)} fusion(f32[1024,2560]{0,1:T(8,128)} %all-gather.8.cloned.1.call-done, f32[1024]{0:T(1024)S(1)} %copy-done.2, f32[1024,160]{0,1:T(8,128)S(1)} %get-tuple-element.55), kind=kOutput, calls=%fused_computation.2 | convolution fusion | flops 5034393600 | bytes 12783616 | tf_op jit(solution)/shard_map/dot_general | solution.py:75
  251.2 2.5 reshape_reshape_reshape.3
  253.7 4.8 copy.28
  258.5 5.7 all-to-all-start
  264.3 33.3 %all-to-all-done = f32[16,160,160]{1,2,0:T(8,128)S(1)} async-done(((f32[16,160,160]{1,2,0:T(8,128)}), f32[16,160,160]{1,2,0:T(8,128)S(1)}, u32[]{:S(2)}, u32[]{:S(2)}) %all-to-all-start) | async-done | bytes 1638432 | tf_op jit(solution)/shard_map/all_to_all | solution.py:39
  299.3 34.5 %all_gather.26 = f32[160,512]{0,1:T(8,128)S(1)} all-gather(f32[160,32]{0,1:T(8,128)S(1)} %copy.33), channel_id=1, replica_groups=mesh['env'=16,'pts_0'=2,'pts_1'=8] {'pts_0','pts_1'}, dimensions={1}, use_global_device_ids=true | all-gather | bytes 348160 | tf_op jit(solution)/shard_map/all_gather | solution.py:104
  334.0 27.8 %all_gather.27 = f32[512,160]{1,0:T(8,128)S(1)} all-gather(f32[32,160]{1,0:T(8,128)S(1)} %slice.144), channel_id=1, replica_groups=mesh['env'=16,'pts_0'=2,'pts_1'=8] {'env'}, dimensions={0}, use_global_device_ids=true | all-gather | bytes 348160 | tf_op jit(solution)/shard_map/all_gather | solution.py:107
  364.2 650.3 %all-gather.10.cloned.1.call-done = f32[8192,32]{1,0:T(8,128)} async-done(((f32[32,32]{1,0:T(8,128)}), f32[8192,32]{1,0:T(8,128)}) %all-gather.10.cloned.1.call-update) | async-done | bytes 1048592 | tf_op jit(solution)/shard_map/all_gather | solution.py:97
  1014.5 5.6 copy.31
  1020.1 3.7 reshape.99
  1024.4 11.7 cholesky.104
  1036.3 9.8 custom-call.30
  1046.7 11.7 cholesky.217
  1058.5 10.0 custom-call.31
  1069.2 11.7 cholesky.238
  1080.9 9.8 custom-call.32
  1091.3 11.7 cholesky.255
  1109.1 11.1 while.4
  1120.2 40.1 %custom-call.34 = f32[4,128,128]{1,2,0:T(8,128)S(1)} custom-call(f32[4,128,128]{2,1,0:T(8,128)} %get-tuple-element.17), custom_call_target="InvertDiagBlocksLowerTriangular" | custom-call | tf_op jit(solution)/shard_map/jit(_solve_triangular)/triangular_solve | solution.py:105
  (81 shorter events, 33.3 us)
Async XLA Ops:
  7.2 69.1 %all-gather.6.cloned.1.call-start = ((), (), s32[]{:S(2)}) async-start(), calls=%async_computation.1 | async-start | bytes 4718592 | tf_op jit(solution)/shard_map/all_gather | solution.py:21
  19.2 218.0 %all-gather.8.cloned.1.call-start = ((), (), s32[]{:S(2)}) async-start(), calls=%async_computation.2 | async-start | bytes 11141120 | tf_op jit(solution)/shard_map/all_gather | solution.py:76
  78.8 158.5 %copy-start.2 = (f32[1024]{0:T(1024)S(1)}, f32[1024]{0:T(1024)}, u32[]{:S(2)}) copy-start(f32[1024]{0:T(1024)} %param.6) | copy-start | bytes 12292
  258.5 39.0 %all-to-all-start = ((f32[16,160,160]{1,2,0:T(8,128)}), f32[16,160,160]{1,2,0:T(8,128)S(1)}, u32[]{:S(2)}, u32[]{:S(2)}) async-start(f32[16,160,160]{1,2,0:T(8,128)} %copy.28), calls=%async_computation | async-start | bytes 5242880 | tf_op jit(solution)/shard_map/all_to_all | solution.py:39
  264.2 750.3 %all-gather.10.cloned.1.call-start = ((), (), s32[]{:S(2)}) async-start(), calls=%async_computation.3 | async-start | bytes 4210688 | tf_op jit(solution)/shard_map/all_gather | solution.py:97
  297.9 1.3 copy-start.1
  361.8 0.8 copy-start
Sparse Core Ops, SparseCore 0:
  19.3 56.9 all-gather.5
  82.8 154.4 all-gather.7
  298.8 715.6 all-gather.9
where the time goes:
time: 1190 us; the launch traced here: 1180 us
  waiting for transfers between devices  872 us (73%)
  other arithmetic  121 us (10%)
  blocking collectives  97.9 us (8%)
  local copies, waits for them, and re-layouts  35.4 us (3%)
  matrix products  28.1 us (2%)
  between operations  17 us (1%)
    all_gather x1, waiting for transfers between devices, local(): lax.all_gather(gram_block[None, :row_block, :col_block], ENV_PTS, axis=0,...  650 us
    all_gather x1, waiting for transfers between devices, local(): lax.all_gather(own_tile, PTS, axis=1, tiled=True)  155 us
    another operation x15, other arithmetic, local(): low_factor = jnp.linalg.cholesky(leading)  79.2 us
    another operation x4, other arithmetic, local(): jax.scipy.linalg.solve_triangular(low_factor, panel_rows.T, lower=True)  40.8 us
    all_gather x1, blocking collectives, local(): lax.all_gather(gram_block[:, :col_block], PTS, axis=1, tiled=True)  34.5 us
    all_gather x1, waiting for transfers between devices, gather_in_order(): blocks = lax.all_gather(blocks, axes[k], axis=0, tiled=True)  33.4 us
    all_to_all x1, waiting for transfers between devices, summed_on_arrival(): lax.all_to_all(cut_along(shard, dim, count), axis, 0, 0, tiled=True)  33.3 us
    all_gather x1, blocking collectives, local(): lax.all_gather(gram_block[:row_block, :], 'env', axis=0, tiled=True)  27.8 us
  transfers between devices with their start and end apart: 4, of which 4 were waited for; matrix products, arithmetic and copies ran while one was open for 0% of the time, Pallas kernels for 0%

commit v1 on v0

--- a/solution.py
+++ b/solution.py
@@ -45,7 +45,7 @@
         features,
         targets,
         (((0,), (1,)), ((), ())),
-        precision=lax.Precision.HIGHEST,
+        precision=lax.Precision.HIGH,
         preferred_element_type=jnp.float32,
     )
     scaled = dots / jnp.sqrt(jnp.float32(features.shape[0]))
@@ -76,7 +76,7 @@
         lax.all_gather(own_tile, PTS, axis=1, tiled=True),
         weighted,
         (((0,), (0,)), ((), ())),
-        precision=lax.Precision.HIGHEST,
+        precision=lax.Precision.HIGH,
         preferred_element_type=jnp.float32,
     )
     partial_gram = partial_gram / jnp.float32(descriptors.shape[1] * env_count)
@@ -94,14 +94,9 @@
     row_ids = local_points(rows_dev, env_rank, env_count, row_block)
     col_ids = local_points(cols_dev, pts_rank, pts_count, col_block)
     gram_block = gram_block + (row_ids[:, None] == col_ids[None, :]).astype(jnp.float32)
-    corner = lax.all_gather(gram_block[None, :row_block, :col_block], ENV_PTS, axis=0, tiled=True)
-    leading = (
-        corner.reshape(env_count, pts_count, row_block, col_block)
-        .transpose(0, 2, 1, 3)
-        .reshape(PANEL, PANEL)
-    )
+    panel_rows = lax.all_gather(gram_block[:, :col_block], PTS, axis=1, tiled=True)
+    leading = lax.all_gather(panel_rows[:row_block], "env", axis=0, tiled=True)
     low_factor = jnp.linalg.cholesky(leading)
-    panel_rows = lax.all_gather(gram_block[:, :col_block], PTS, axis=1, tiled=True)
     row_factor = jax.scipy.linalg.solve_triangular(low_factor, panel_rows.T, lower=True).T
     panel_out = lax.dynamic_slice_in_dim(row_factor, pts_rank * col_block, col_block, 1)
     top_rows = lax.all_gather(gram_block[:row_block, :], "env", axis=0, tiled=True)

time: 1190 us -> 528 us (0.44)
  waiting for transfers between devices: 872 us -> 229 us
    all_gather x1, waiting for transfers between devices: 650 us -> 7.63 us  [local(): leading = lax.all_gather(panel_rows[:row_block], 'env', axis=0, tiled=True)]
where the time goes in v1:
time: 528 us; the launch traced here: 521 us
  waiting for transfers between devices  229 us (43%)
  other arithmetic  122 us (23%)
  blocking collectives  98.2 us (19%)
  local copies, waits for them, and re-layouts  25.6 us (5%)
  matrix products  23.2 us (4%)
  between operations  17 us (3%)
  starting transfers between devices  5.8 us (1%)
    all_gather x1, waiting for transfers between devices, local(): lax.all_gather(own_tile, PTS, axis=1, tiled=True)  155 us
    another operation x15, other arithmetic, local(): low_factor = jnp.linalg.cholesky(leading)  79.5 us
    another operation x4, other arithmetic, local(): jax.scipy.linalg.solve_triangular(low_factor, panel_rows.T, lower=True)  40.8 us
    all_gather x1, blocking collectives, local(): lax.all_gather(gram_block[:, :col_block], PTS, axis=1, tiled=True)  34.4 us
    all_gather x1, waiting for transfers between devices, gather_in_order(): blocks = lax.all_gather(blocks, axes[k], axis=0, tiled=True)  33.4 us
    all_to_all x1, waiting for transfers between devices, summed_on_arrival(): lax.all_to_all(cut_along(shard, dim, count), axis, 0, 0, tiled=True)  33.3 us
    all_gather x1, blocking collectives, local(): lax.all_gather(gram_block[:row_block, :], 'env', axis=0, tiled=True)  28.2 us
    all_gather x1, blocking collectives, local(): own_points = lax.all_gather(points, 'env', axis=1, tiled=True)  23.6 us
  transfers between devices with their start and end apart: 4, of which 4 were waited for; matrix products, arithmetic and copies ran while one was open for 0% of the time, Pallas kernels for 0%

profile of v1, /device:TPU:1, one launch (start us, length us, event | category | flops | bytes accessed | tf_op | source)
XLA Modules:
  0.0 520.9 jit_solution(16651984961840194268)
XLA Ops:
  7.2 12.0 %all-gather = f32[128,1024]{1,0:T(8,128)} all-gather(f32[64,1024]{1,0:T(8,128)} %param.5), channel_id=2, replica_groups=mesh['env'=16,'pts_0'=2,'pts_1'=8] {'pts_0'}, dimensions={0}, use_global_device_ids=true | all-gather | bytes 786432 | tf_op jit(solution)/shard_map/all_gather | solution.py:21
  19.3 23.6 %all_gather.23 = f32[160,1024]{0,1:T(8,128)S(1)} all-gather(f32[160,64]{0,1:T(8,128)} %param.7), channel_id=1, replica_groups=mesh['env'=16,'pts_0'=2,'pts_1'=8] {'env'}, dimensions={1}, use_global_device_ids=true | all-gather | bytes 696320 | tf_op jit(solution)/shard_map/all_gather | solution.py:66
  42.9 33.4 %all-gather.5.cloned.1.call-done = f32[16,64,1024]{2,1,0:T(8,128)} async-done(((f32[2,64,1024]{2,1,0:T(8,128)}), f32[16,64,1024]{2,1,0:T(8,128)}) %all-gather.5.cloned.1.call-update) | async-done | bytes 4194320 | tf_op jit(solution)/shard_map/all_gather | solution.py:21
  76.3 2.5 copy.28
  78.8 2.3 multiply_multiply_fusion
  81.1 154.6 %all-gather.7.cloned.1.call-done = f32[1024,2560]{0,1:T(8,128)} async-done(((f32[1024,160]{0,1:T(8,128)}), f32[1024,2560]{0,1:T(8,128)}) %all-gather.7.cloned.1.call-update) | async-done | bytes 10485776 | tf_op jit(solution)/shard_map/all_gather | solution.py:76
  235.7 10.6 %convolution_multiply_fusion = f32[2560,160]{0,1:T(8,128)} fusion(f32[1024,2560]{0,1:T(8,128)} %all-gather.7.cloned.1.call-done, f32[1024]{0:T(1024)S(1)} %copy-done.2, f32[1024,160]{0,1:T(8,128)S(1)} %get-tuple-element.55), kind=kOutput, calls=%fused_computation.2 | convolution fusion | flops 2517811200 | bytes 12783616 | tf_op jit(solution)/shard_map/dot_general | solution.py:75
  246.3 2.6 reshape_reshape_reshape.3
  248.9 3.0 copy.29
  251.9 5.7 %all-to-all-start = ((f32[16,160,160]{1,2,0:T(8,128)}), f32[16,160,160]{1,2,0:T(8,128)S(1)}, u32[]{:S(2)}, u32[]{:S(2)}) async-start(f32[16,160,160]{1,2,0:T(8,128)} %copy.29), calls=%async_computation | async-start | bytes 5242880 | tf_op jit(solution)/shard_map/all_to_all | solution.py:39
  257.6 33.3 %all-to-all-done = f32[16,160,160]{1,2,0:T(8,128)S(1)} async-done(((f32[16,160,160]{1,2,0:T(8,128)}), f32[16,160,160]{1,2,0:T(8,128)S(1)}, u32[]{:S(2)}, u32[]{:S(2)}) %all-to-all-start) | async-done | bytes 1638432 | tf_op jit(solution)/shard_map/all_to_all | solution.py:39
  291.4 34.4 %all_gather.25 = f32[160,512]{0,1:T(8,128)S(1)} all-gather(f32[160,32]{0,1:T(8,128)S(1)} %copy.31), channel_id=1, replica_groups=mesh['env'=16,'pts_0'=2,'pts_1'=8] {'pts_0','pts_1'}, dimensions={1}, use_global_device_ids=true | all-gather | bytes 348160 | tf_op jit(solution)/shard_map/all_gather | solution.py:97
  327.3 28.2 %all_gather.27 = f32[512,160]{1,0:T(8,128)S(1)} all-gather(f32[32,160]{1,0:T(8,128)S(1)} %slice.144), channel_id=1, replica_groups=mesh['env'=16,'pts_0'=2,'pts_1'=8] {'env'}, dimensions={0}, use_global_device_ids=true | all-gather | bytes 348160 | tf_op jit(solution)/shard_map/all_gather | solution.py:102
  358.0 7.6 %all-gather.9.cloned.1.call-done = f32[512,512]{1,0:T(8,128)} async-done(((f32[32,512]{1,0:T(8,128)}), f32[512,512]{1,0:T(8,128)}) %all-gather.9.cloned.1.call-update) | async-done | bytes 1048592 | tf_op jit(solution)/shard_map/all_gather | solution.py:98
  368.7 11.7 %cholesky.104 = f32[128,128]{1,0:T(8,128)S(1)} custom-call(f32[128,128]{1,0:T(8,128)S(1)} %cholesky.266), custom_call_target="Cholesky" | custom-call | tf_op jit(solution)/shard_map/jit(cholesky)/cholesky | solution.py:99
  380.5 9.8 %custom-call.30 = f32[1,128,128]{1,2,0:T(8,128)S(1)} custom-call(f32[1,128,128]{2,1,0:T(8,128)S(1)} %get-tuple-element.53), custom_call_target="InvertDiagBlocksLowerTriangular" | custom-call | tf_op jit(solution)/shard_map/jit(cholesky)/cholesky | solution.py:99
  391.0 11.7 %cholesky.217 = f32[128,128]{1,0:T(8,128)S(1)} custom-call(f32[128,128]{1,0:T(8,128)S(1)} %cholesky.270), custom_call_target="Cholesky" | custom-call | tf_op jit(solution)/shard_map/jit(cholesky)/cholesky | solution.py:99
  402.8 10.0 %custom-call.31 = f32[1,128,128]{1,2,0:T(8,128)S(1)} custom-call(f32[1,128,128]{2,1,0:T(8,128)S(1)} %get-tuple-element.50), custom_call_target="InvertDiagBlocksLowerTriangular" | custom-call | tf_op jit(solution)/shard_map/jit(cholesky)/cholesky | solution.py:99
  413.4 11.7 %cholesky.238 = f32[128,128]{1,0:T(8,128)S(1)} custom-call(f32[128,128]{1,0:T(8,128)S(1)} %cholesky.275), custom_call_target="Cholesky" | custom-call | tf_op jit(solution)/shard_map/jit(cholesky)/cholesky | solution.py:99
  425.2 9.8 %custom-call.32 = f32[1,128,128]{1,2,0:T(8,128)S(1)} custom-call(f32[1,128,128]{2,1,0:T(8,128)S(1)} %get-tuple-element.47), custom_call_target="InvertDiagBlocksLowerTriangular" | custom-call | tf_op jit(solution)/shard_map/jit(cholesky)/cholesky | solution.py:99
  435.6 11.9 %cholesky.255 = f32[128,128]{1,0:T(8,128)S(1)} custom-call(f32[128,128]{1,0:T(8,128)S(1)} %convolution_subtract_fusion.9), custom_call_target="Cholesky" | custom-call | tf_op jit(solution)/shard_map/jit(cholesky)/cholesky | solution.py:99
  453.5 10.9 %while.4 = (s32[]{:T(128)}, f32[512,512]{1,0:T(8,128)S(1)}, s32[4,2]{0,1:T(2,128)S(1)}, f32[4,128,128]{2,1,0:T(8,128)}, s32[]{:T(128)}) while((s32[]{:T(128)}, f32[512,512]{1,0:T(8,128)S(1)}, s32[4,2]{0,1:T(2,128)S(1)}, f32[4,128,128]{2,1,0:T(8,128)}, s32[]{:T(128)}) %tuple.45), condition=%wide.while_cond, body=%wide.while_body.sunk | while | flops 2 | bytes 132205 | solution.py:100
  456.9 2.1 bitcast_dynamic-update-slice_fusion.2
  464.4 40.1 %custom-call.34 = f32[4,128,128]{1,2,0:T(8,128)S(1)} custom-call(f32[4,128,128]{2,1,0:T(8,128)} %get-tuple-element.17), custom_call_target="InvertDiagBlocksLowerTriangular" | custom-call | tf_op jit(solution)/shard_map/jit(_solve_triangular)/triangular_solve | solution.py:100
  (80 shorter events, 31.3 us)
Async XLA Ops:
  7.2 69.1 %all-gather.5.cloned.1.call-start = ((), (), s32[]{:S(2)}) async-start(), calls=%async_computation.1 | async-start | bytes 4718592 | tf_op jit(solution)/shard_map/all_gather | solution.py:21
  19.2 216.5 %all-gather.7.cloned.1.call-start = ((), (), s32[]{:S(2)}) async-start(), calls=%async_computation.2 | async-start | bytes 11141120 | tf_op jit(solution)/shard_map/all_gather | solution.py:76
  78.8 156.9 %copy-start.2 = (f32[1024]{0:T(1024)S(1)}, f32[1024]{0:T(1024)}, u32[]{:S(2)}) copy-start(f32[1024]{0:T(1024)} %param.6) | copy-start | bytes 12292
  251.9 39.1 %all-to-all-start = ((f32[16,160,160]{1,2,0:T(8,128)}), f32[16,160,160]{1,2,0:T(8,128)S(1)}, u32[]{:S(2)}, u32[]{:S(2)}) async-start(f32[16,160,160]{1,2,0:T(8,128)} %copy.29), calls=%async_computation | async-start | bytes 5242880 | tf_op jit(solution)/shard_map/all_to_all | solution.py:39
  257.6 108.1 %all-gather.9.cloned.1.call-start = ((), (), s32[]{:S(2)}) async-start(), calls=%async_computation.3 | async-start | bytes 1114112 | tf_op jit(solution)/shard_map/all_gather | solution.py:98
  291.3 66.7 %copy-start.1 = (f32[160,160]{1,0:T(8,128)}, f32[160,160]{1,0:T(8,128)S(1)}, u32[]{:S(2)}) copy-start(f32[160,160]{1,0:T(8,128)S(1)} %convert_add_fusion) | copy-start | bytes 307204
  355.6 0.8 copy-start
Sparse Core Ops, SparseCore 0:
  19.3 56.9 all-gather.4
  81.2 154.4 all-gather.6
  326.7 38.8 all-gather.8

commit v2 on v1

v2 whole, which is shorter than its diff:
```python
import functools

import jax
import jax.numpy as jnp
from jax import lax
from jax.experimental import pallas as pl
from jax.experimental.pallas import tpu as pltpu
from jax.sharding import PartitionSpec as P

MESH = pl.DeviceIdType.MESH
HI = lax.Precision.HIGHEST
F32 = jnp.float32
BF16 = jnp.bfloat16
NB = 128
NENV = 16384
OFFSETS = (0, 1, 2, 4)


def placed():
    e, p = lax.axis_index("env"), lax.axis_index("pts")
    x, y_lo, c = e // 4, (e // 2) % 2, e % 2
    y_hi, z = p // 8, p % 8
    return e, p, x, 2 * y_hi + y_lo, z, c


def device(x, y, z, c):
    return (4 * x + 2 * (y % 2) + c, 8 * (y // 2) + z)


def remote(src, dst, send_sem, recv_sem, to):
    return pltpu.make_async_remote_copy(
        src_ref=src, dst_ref=dst, send_sem=send_sem, recv_sem=recv_sem, device_id=to, device_id_type=MESH
    )


def arrived(ref, sem):
    pltpu.make_async_copy(ref, ref, sem).wait()


def halves(a):
    hi = a.astype(BF16)
    return hi, (a - hi.astype(F32)).astype(BF16)


def dot3(a, b, dims):
    one = lambda l, r: lax.dot_general(l, r, (dims, ((), ())), preferred_element_type=F32)
    return one(a[0], b[0]) + (one(a[0], b[1]) + one(a[1], b[0]))


def gather_and_multiply(
    desc, points, weight, tt_out, panel_out,
    half, other_weight, line, table, feats, feats_hi, feats_lo, rows_hi, rows_lo, kp, kt,
    half_s, half_r, swap_s, swap_r, local_s, zp_s, zp_r, zt_s, zt_r, slab_s, slab_r, slabx_s, slabx_r,
    ring_s, ring_r, ringx_s, ringx_r,
):
    e, p, x, y, z, c = placed()
    h = p // 8
    native = c == h
    turn = jnp.where(native, 1, 7)
    sibling = device(x, y, z, 1 - c)
    partner = device(x, (y + 2) % 4, z, 1 - c)
    along_z = lambda d: device(x, y, (z + d) % 8, c)

    def step(j1, j2):
        return (x + j1 * (1 - c) + j2 * c) % 4, (y + j1 * c + j2 * (1 - c)) % 4

    def slab_of(j1, j2, core):
        sx = (x + 8 - j1 * (1 - core) - j2 * core) % 4
        sy = (y + 8 - j1 * core - j2 * (1 - core)) % 4
        lanes = pl.multiple_of(128 * (2 * sx + sy % 2), 128)
        return table.at[sy // 2, core, :, pl.ds(lanes, 128)]

    barrier = pltpu.get_barrier_semaphore()
    greet = [sibling, partner] + [along_z(d) for d in range(1, 8)]
    greet += [device(*step(j, 0), z, c) for j in (1, 2, 3)] + [device(*step(0, j), z, c) for j in (1, 2, 3)]
    for who in greet:
        pl.semaphore_signal(barrier, inc=1, device_id=who, device_id_type=MESH)
    pl.semaphore_wait(barrier, len(greet))

    o = 1 - c
    to_sibling = [
        remote(points.at[pl.ds(pl.multiple_of(16 * o, 16), 16)], half.at[0:16], half_s.at[0], half_r.at[0], sibling),
        remote(points.at[pl.ds(pl.multiple_of(32 + 64 * o, 32), 64)], half.at[16:80], half_s.at[1], half_r.at[1], sibling),
        remote(weight, other_weight, half_s.at[2], half_r.at[2], sibling),
    ]
    for copy in to_sibling:
        copy.start()
    swap = remote(desc, feats.at[p], swap_s, swap_r, partner)
    keep = pltpu.make_async_copy(desc, feats.at[p], swap_r)

    @pl.when(native)
    def _():
        keep.start()

    @pl.when(jnp.logical_not(native))
    def _():
        swap.start()

    arrived(half.at[0:16], half_r.at[0])
    arrived(half.at[16:80], half_r.at[1])
    mine = jnp.concatenate(
        [points[pl.ds(pl.multiple_of(16 * c, 16), 16)], points[pl.ds(pl.multiple_of(32 + 64 * c, 32), 64)]], axis=0
    )
    theirs = half[...]
    packed = jnp.where(c == 0, jnp.concatenate([mine, theirs], axis=1), jnp.concatenate([theirs, mine], axis=1))
    own_panel = line.at[pl.ds(pl.multiple_of(16 * z, 16), 16)]
    line[pl.ds(pl.multiple_of(16 * z, 16), 16)] = packed[0:16]
    line[128:192] = packed[16:80]

    lined = []
    for s in (1, 2, 3):
        rows = pl.ds(128 + 64 * s, 64)
        lined.append(remote(line.at[128:192], line.at[rows], zt_s.at[s], zt_r.at[s], along_z(8 - OFFSETS[s])))
    for d in range(1, 8):
        lined.append(remote(own_panel, own_panel, zp_s.at[d], zp_r.at[d], along_z(d)))
    for copy in lined:
        copy.start()

    def piece(m, core, sign):
        d = (0, 1, 2, 3, 4, 7, 6, 5)[m]
        return feats.at[8 * core + (z + 8 * 8 - sign * d) % 8]

    rings, across = [], []

    def pass_on(m):
        src = piece(m, c, turn)
        if m in (0, 1, 2, 3):
            copy = remote(src, src, ring_s.at[m + 1], ring_r.at[m + 1], along_z(turn))
            copy.start()
            rings.append(copy)
        if m in (0, 5, 6):
            n = 5 if m == 0 else m + 1
            copy = remote(src, src, ring_s.at[n], ring_r.at[n], along_z(8 - turn))
            copy.start()
            rings.append(copy)
        copy = remote(src, src, ringx_s.at[m], ringx_r.at[m], sibling)
        copy.start()
        across.append(copy)

    arrived(piece(0, c, turn), swap_r)
    pass_on(0)

    for s in (1, 2, 3):
        arrived(line.at[pl.ds(128 + 64 * s, 64)], zt_r.at[s])
    for d in range(1, 8):
        rows = pl.ds(pl.multiple_of(16 * ((z + 8 - d) % 8), 16), 16)
        arrived(line.at[rows], zp_r.at[d])

    slabs = []

    def spread(j1, src, dst):
        if j1 == 0:
            for j in (1, 2, 3):
                slabs.append(remote(src, dst, slab_s.at[4 * j], slab_r.at[4 * j], device(*step(j, 0), z, c)))
                slabs[-1].start()
        for j in (1, 2, 3):
            n = 4 * j1 + j
            slabs.append(remote(src, dst, slab_s.at[n], slab_r.at[n], device(*step(0, j), z, c)))
            slabs[-1].start()

    def to_other_core(n, src, dst):
        slabs.append(remote(src, dst, slabx_s.at[n], slabx_r.at[n], sibling))
        slabs[-1].start()

    own = slab_of(0, 0, c)
    spread(0, line, own)
    to_other_core(0, line, own)
    stay = pltpu.make_async_copy(line, own, local_s)
    stay.start()

    def take_piece(m):
        arrived(piece(m, c, turn), ring_r.at[m])
        pass_on(m)

    def take_slab(j1, j2):
        here = slab_of(j1, j2, c)
        arrived(here, slab_r.at[4 * j1 + j2])
        if j2 == 0:
            spread(j1, here, here)
        to_other_core(4 * j1 + j2, here, here)

    take_slab(1, 0)
    take_slab(3, 0)
    take_piece(1)
    take_piece(5)
    take_slab(2, 0)
    take_slab(0, 1)
    take_slab(0, 3)
    take_slab(0, 2)
    take_piece(2)
    take_piece(6)
    for j1 in (1, 3):
        for j2 in (1, 3, 2):
            take_slab(j1, j2)
    take_piece(3)
    take_piece(7)
    for j2 in (1, 3, 2):
        take_slab(2, j2)
    take_piece(4)

    for m in range(8):
        arrived(piece(m, o, 8 - turn), ringx_r.at[m])
    for j1 in range(4):
        for j2 in range(4):
            arrived(slab_of(j1, j2, o), slabx_r.at[4 * j1 + j2])
    stay.wait()
    arrived(other_weight, half_r.at[2])
    for copy in to_sibling + lined + rings + across + slabs:
        copy.wait_send()

    @pl.when(jnp.logical_not(native))
    def _():
        swap.wait_send()

    def split_feats(i, carry):
        hi, lo = halves(feats[i])
        rows = pl.ds(pl.multiple_of(64 * i, 64), 64)
        feats_hi[rows] = hi
        feats_lo[rows] = lo
        return carry

    lax.fori_loop(0, 16, split_feats, 0)

    def kernel_rows(i, carry):
        hh, cc = i // 2, i % 2
        hi, lo = halves(table[hh, cc, 0:256])
        rows_hi[0:256], rows_lo[0:256] = hi, lo
        hi, lo = halves(table[hh, cc, pl.ds(pl.multiple_of(256 + 64 * c, 64), 64)])
        rows_hi[256:320], rows_lo[256:320] = hi, lo

        def columns(t, carry):
            lanes = pl.ds(pl.multiple_of(256 * t, 256), 256)
            scaled = dot3(
                (rows_hi[...], rows_lo[...]), (feats_hi[:, lanes], feats_lo[:, lanes]), ((1,), (0,))
            ) * (1.0 / 32.0)
            value = 0.25 * scaled * scaled * scaled
            for zz in range(8):
                at = pl.multiple_of(256 * hh + 32 * zz + 16 * cc, 16)
                kp[pl.ds(at, 16), lanes] = value[16 * zz : 16 * zz + 16]
            for s in range(3):
                at = pl.multiple_of(128 * hh + 64 * cc, 64)
                kt[s, pl.ds(at, 64), lanes] = value[128 + 64 * s : 192 + 64 * s]
            return carry

        lax.fori_loop(0, 4, columns, 0)
        return carry

    lax.fori_loop(0, 4, kernel_rows, 0)

    w = jnp.where(native, weight[0:1], other_weight[0:1]) * (1.0 / NENV)
    nt = ((1,), (1,))

    def unit(k, carry):
        first = (k + 1) // 2
        row = jnp.where(first == 1, c, 0)
        col = jnp.where(first == 0, 0, jnp.where(first == 1, 1 + c, 2))
        side = jnp.where(first == 0, c, (k + 1) % 2)
        a = halves(kt[row] * w)
        b = halves(kt[col, pl.ds(pl.multiple_of(128 * side, 128), 128)])
        tt_out[k] = dot3(a, b, nt)
        return carry

    lax.fori_loop(0, 5, unit, 0)
    trail = halves(kt[0, pl.ds(pl.multiple_of(128 * c, 128), 128)] * w)
    lead = halves(kp[pl.ds(pl.multiple_of(256 * c + 32 * z, 32), 32)] * w)

    def panel(i, carry):
        a = halves(kp[pl.ds(pl.multiple_of(128 * i, 128), 128)])
        panel_out[pl.ds(4 * i, 4), :, 0:128] = dot3(a, trail, nt).reshape(4, 32, 128)
        corner = jnp.concatenate([dot3(a, lead, nt), jnp.zeros((128, 96), F32)], axis=1)
        panel_out[pl.ds(4 * i, 4), :, 128:256] = corner.reshape(4, 32, 128)
        return carry

    lax.fori_loop(0, 4, panel, 0)


def kernel_gram(desc, points, weight):
    dma = pltpu.SemaphoreType.DMA
    vmem = pl.BlockSpec(memory_space=pltpu.VMEM)
    return pl.pallas_call(
        gather_and_multiply,
        out_shape=(jax.ShapeDtypeStruct((5, 256, 128), F32), jax.ShapeDtypeStruct((16, 32, 256), F32)),
        in_specs=[vmem] * 3,
        out_specs=[vmem] * 2,
        scratch_shapes=[
            pltpu.VMEM((80, 64), F32),
            pltpu.VMEM((8, 1024), F32),
            pltpu.VMEM((384, 128), F32),
            pltpu.VMEM((2, 2, 384, 1024), F32),
            pltpu.VMEM((16, 64, 1024), F32),
            pltpu.VMEM((1024, 1024), BF16),
            pltpu.VMEM((1024, 1024), BF16),
            pltpu.VMEM((320, 1024), BF16),
            pltpu.VMEM((320, 1024), BF16),
            pltpu.VMEM((512, 1024), F32),
            pltpu.VMEM((3, 256, 1024), F32),
            dma((3,)), dma((3,)), dma, dma, dma,
            dma((8,)), dma((8,)), dma((4,)), dma((4,)),
            dma((16,)), dma((16,)), dma((16,)), dma((16,)),
            dma((8,)), dma((8,)), dma((8,)), dma((8,)),
        ],
        compiler_params=pltpu.CompilerParams(collective_id=0, has_side_effects=True, vmem_limit_bytes=60 * 2**20),
    )(desc, points, weight)


def reduce_and_share(
    tt, pp, corner, p_rows, p_cols, block,
    p_in, tt_in, t_own, c_own, tt_own,
    p_s, p_r, tt_s, tt_r, col_s, col_r, row_s, row_r, cor_s, cor_r, blk_s, blk_r,
):
    e, p, x, y, z, c = placed()
    h = p // 8
    me = 4 * x + y
    barrier = pltpu.get_barrier_semaphore()

    def is_me(to):
        return (to[0] == e) & (to[1] == p)

    def greet(who):
        @pl.when(jnp.logical_not(is_me(who)))
        def _():
            pl.semaphore_signal(barrier, inc=1, device_id=who, device_id_type=MESH)

    def send(src, dst, send_sem, recv_sem, to, also=None):
        here, there = is_me(to), jnp.logical_not(is_me(to))
        if also is not None:
            here, there = here & also, there & also

        @pl.when(here)
        def _():
            pltpu.make_async_copy(src, dst, recv_sem).start()

        @pl.when(there)
        def _():
            remote(src, dst, send_sem, recv_sem, to).start()

        def finish():
            @pl.when(there)
            def _():
                remote(src, dst, send_sem, recv_sem, to).wait_send()

        return finish

    z_row, z_col = e % 8, z
    apart = (z_col + 8 - z_row) % 8
    straight = apart <= 4
    gap = jnp.where(straight, apart, 8 - apart)
    z_first = jnp.where(straight, z_row, z_col)
    h_first = jnp.where(straight, e // 8, h)
    h_second = jnp.where(straight, h, e // 8)
    z_from = (z_first + 8 - jnp.where(gap == 3, 1, 0)) % 8
    c_from = jnp.where(gap == 0, h_second, jnp.where(gap >= 3, 1, 0))

    for q in range(16):
        greet(device(q // 4, q % 4, z, h))
        greet(device(q // 4, q % 4, z, c))
        greet((q, p))
        greet((q, e))
    for t in range(8):
        q = 8 * h_first + t
        greet(device(q // 4, q % 4, z_from, c_from))

    owners = []
    for k in range(5):
        first = (k + 1) // 2
        d_row = c if first == 1 else 0
        d_col = (0, 1 + 3 * c, 2 + 2 * c)[first]
        side = c if k == 0 else (k + 1) % 2
        p_a = 8 * (me // 8) + (z + d_row) % 8
        p_b = 8 * side + (z + d_col) % 8
        owners.append((2 * k, k, (p_a, p_b), None))
        if k > 0:
            owners.append((2 * k + 1, k, (p_b, p_a), None if first == 1 else c == 0))

    targets = [(a, 8 * c + z) for a in range(16)] + [device(q // 4, q % 4, z, c) for q in range(16)]
    targets += [(p, q) for q in range(16)] + [(q, p) for q in range(16)]
    expected = 0
    for to in targets:
        expected = expected + jnp.where(is_me(to), 0, 1)
    for _, _, to, also in owners:
        counts = jnp.logical_not(is_me(to)) if also is None else jnp.logical_not(is_me(to)) & also
        expected = expected + jnp.where(counts, 1, 0)
    pl.semaphore_wait(barrier, expected)

    pending = []
    for a in range(16):
        pending.append(send(pp.at[a], p_in.at[me], p_s.at[a], p_r.at[me], (a, 8 * c + z)))
    for q in range(16):
        to = device(q // 4, q % 4, z, c)
        pending.append(send(tt.at[:, 16 * q : 16 * q + 16], tt_in.at[me], tt_s.at[q], tt_r.at[me], to))

    for q in range(16):
        arrived(p_in.at[q], p_r.at[q])
    total = p_in[0]
    for q in range(1, 16):
        total = total + p_in[q]
    at = lax.broadcasted_iota(jnp.int32, (32, 256), 1)
    one = (at == 128 + lax.broadcasted_iota(jnp.int32, (32, 256), 0)) & (e == p)
    t_own[...] = total + jnp.where(one, 1.0, 0.0)
    for q in range(16):
        pending.append(send(t_own, p_rows.at[e], row_s.at[q], row_r.at[e], (p, q)))
    for q in range(16):
        pending.append(send(t_own, p_cols.at[e], col_s.at[q], col_r.at[e], (q, p)))

    for q in range(16):
        arrived(p_rows.at[q], row_r.at[q])
    for q in range(4):
        strip = p_rows[4 * q : 4 * q + 4, :, 128:256].reshape(128, 128)
        c_own[:, 128 * q : 128 * q + 128] = jnp.transpose(strip)[0:32]
    for q in range(16):
        pending.append(send(c_own, corner.at[e], cor_s.at[q], cor_r.at[e], (q, p)))

    for q in range(16):
        arrived(tt_in.at[q], tt_r.at[q])
    total = tt_in[0]
    for q in range(1, 16):
        total = total + tt_in[q]
    tt_own[...] = total
    part = me % 8
    rows = pl.ds(pl.multiple_of(16 * part, 16), 16)
    for n, k, to, also in owners:
        pending.append(send(tt_own.at[k], block.at[rows], blk_s.at[n], blk_r.at[part], to, also))

    for q in range(16):
        arrived(p_cols.at[q], col_r.at[q])
        arrived(corner.at[q], cor_r.at[q])
    for t in range(8):
        arrived(block.at[16 * t : 16 * t + 16], blk_r.at[t])
    for finish in pending:
        finish()


def share(tt, pp):
    dma = pltpu.SemaphoreType.DMA
    vmem = pl.BlockSpec(memory_space=pltpu.VMEM)
    return pl.pallas_call(
        reduce_and_share,
        out_shape=(
            jax.ShapeDtypeStruct((16, 32, 512), F32),
            jax.ShapeDtypeStruct((16, 32, 256), F32),
            jax.ShapeDtypeStruct((16, 32, 256), F32),
            jax.ShapeDtypeStruct((128, 128), F32),
        ),
        in_specs=[vmem] * 2,
        out_specs=[vmem] * 4,
        scratch_shapes=[
            pltpu.VMEM((16, 32, 256), F32),
            pltpu.VMEM((16, 5, 16, 128), F32),
            pltpu.VMEM((32, 256), F32),
            pltpu.VMEM((32, 512), F32),
            pltpu.VMEM((5, 16, 128), F32),
        ]
        + [dma((16,))] * 12,
        compiler_params=pltpu.CompilerParams(collective_id=1, has_side_effects=True, vmem_limit_bytes=32 * 2**20),
    )(tt, pp)


def dot_hi(a, b, dims):
    return lax.dot_general(a, b, (dims, ((), ())), precision=HI, preferred_element_type=F32)


def inverse_factor(d_ref, e_ref):
    rows = lax.broadcasted_iota(jnp.int32, (8, NB), 0)
    lanes = lax.broadcasted_iota(jnp.int32, (8, NB), 1)
    groups = NB // 8
    full = lambda v: jnp.broadcast_to(v, (8, NB))
    for g in range(groups):
        e_ref[8 * g : 8 * g + 8, :] = (lanes == rows + 8 * g).astype(F32)
    for t in range(groups):
        v = d_ref[8 * t : 8 * t + 8, :]
        e = e_ref[8 * t : 8 * t + 8, :]
        c = [full(v[:, 8 * t + i : 8 * t + i + 1]) for i in range(8)]
        v_row, e_row, c_row, inv = [], [], [], []
        pivots = jnp.ones((8, NB), F32)
        for i in range(8):
            pivot = full(c[i][i : i + 1])
            pivots = jnp.where(rows == i, pivot, pivots)
            r = 1.0 / pivot
            inv.append(r)
            v_row.append(full(v[i : i + 1]))
            e_row.append(full(e[i : i + 1]))
            c_row.append([full(c[k][i : i + 1]) if k > i else None for k in range(8)])
            if i < 7:
                m = jnp.where(rows > i, c[i] * r, 0.0)
                for k in range(i + 1, 8):
                    c[k] = c[k] - m * c_row[i][k]
                v = v - m * v_row[i]
                e = e - m * e_row[i]
        e_ref[8 * t : 8 * t + 8, :] = e * lax.rsqrt(pivots)
        for g in range(t + 1, groups):
            v = d_ref[8 * g : 8 * g + 8, :]
            e = e_ref[8 * g : 8 * g + 8, :]
            c = [full(v[:, 8 * t + i : 8 * t + i + 1]) for i in range(8)]
            for i in range(8):
                m = c[i] * inv[i]
                for k in range(i + 1, 8):
                    c[k] = c[k] - m * c_row[i][k]
                v = v - m * v_row[i]
                e = e - m * e_row[i]
            d_ref[8 * g : 8 * g + 8, :] = v
            e_ref[8 * g : 8 * g + 8, :] = e


def factor_and_update(where, corner, p_rows, p_cols, block, panel_ref, trail_ref, a, ui, uj, d, inv_ref):
    e, p = where[0], where[1]
    n = a.shape[0]
    a[...] = corner[...].reshape(n, n)
    ui[...] = p_rows[...].reshape(n, 256)
    uj[...] = p_cols[:, :, 0:128].reshape(n, 128)
    for k in range(n // NB):
        lo, hi = k * NB, (k + 1) * NB
        d[...] = a[lo:hi, lo:hi]
        inverse_factor(d, inv_ref)
        inv = inv_ref[...]
        ui[lo:hi, :] = dot_hi(inv, ui[lo:hi, :], ((1,), (0,)))
        uj[lo:hi, :] = dot_hi(inv, uj[lo:hi, :], ((1,), (0,)))
        if hi < n:
            a[lo:hi, hi:] = dot_hi(inv, a[lo:hi, hi:], ((1,), (0,)))
            u = a[lo:hi, hi:]
            a[hi:, hi:] -= dot_hi(u, u, ((0,), (0,)))
            ui[hi:, :] -= dot_hi(u, ui[lo:hi, :], ((0,), (0,)))
            uj[hi:, :] -= dot_hi(u, uj[lo:hi, :], ((0,), (0,)))
    gram = block[...]
    straight = (p % 8 + 8 - e % 8) % 8 <= 4
    gram = jnp.where(straight, gram, jnp.transpose(gram))
    same = lax.broadcasted_iota(jnp.int32, (128, 128), 0) == lax.broadcasted_iota(jnp.int32, (128, 128), 1)
    gram = gram + jnp.where(same & (e == p), 1.0, 0.0)
    trail_ref[...] = gram - dot_hi(ui[:, 0:128], uj[...], ((0,), (0,)))
    strip = jnp.transpose(ui[pl.ds(pl.multiple_of(32 * p, 32), 32), :])
    panel_ref[0:32, :] = strip[128:160]
    panel_ref[32:160, :] = strip[0:128]


def factor(where, corner, p_rows, p_cols, block):
    vmem = pl.BlockSpec(memory_space=pltpu.VMEM)
    return pl.pallas_call(
        factor_and_update,
        out_shape=(jax.ShapeDtypeStruct((160, 32), F32), jax.ShapeDtypeStruct((128, 128), F32)),
        in_specs=[pl.BlockSpec(memory_space=pltpu.SMEM)] + [vmem] * 4,
        out_specs=[vmem] * 2,
        scratch_shapes=[
            pltpu.VMEM((512, 512), F32),
            pltpu.VMEM((512, 256), F32),
            pltpu.VMEM((512, 128), F32),
            pltpu.VMEM((NB, NB), F32),
            pltpu.VMEM((NB, NB), F32),
        ],
    )(where, corner, p_rows, p_cols, block)


def local(descriptors, env_weight, points):
    weight = jnp.broadcast_to(env_weight[None, :], (8, env_weight.shape[0]))
    tt, pp = kernel_gram(descriptors, points, weight)
    shared = share(tt, pp)
    where = jnp.stack([lax.axis_index("env"), lax.axis_index("pts")]).astype(jnp.int32)
    return factor(where, *shared)


def solution(mesh):
    return jax.shard_map(
        local,
        mesh=mesh,
        in_specs=(P("pts", "env"), P("env"), P("pts", "env")),
        out_specs=(P("env", "pts"), P("env", "pts")),
        check_vma=False,
    )
```

time: 528 us -> 162 us (0.31); the launches traced: 521 us -> 162 us
  waiting for transfers between devices: 229 us -> 0 us
  Pallas kernels: 0 us -> 151 us
  other arithmetic: 122 us -> 0.58 us
  blocking collectives: 98.2 us -> 0 us
  matrix products: 23.2 us -> 0 us
  local copies, waits for them, and re-layouts: 25.6 us -> 9.09 us
  between operations: 17 us -> 0.68 us
  starting transfers between devices: 5.8 us -> 0 us
    all_gather x3 -> x0, waiting for transfers between devices: 196 us -> none  [the longest x1 155 us: local(): lax.all_gather(own_tile, PTS, axis=1, tiled=True)]
    pallas_call x0 -> x3, Pallas kernels: none -> 151 us  [the longest x1 71.6 us: kernel_gram(): pl.pallas_call(gather_and_multiply, out_shape=(jax.ShapeDtypeStruct((5, 2...]
    another operation x19 -> x1, other arithmetic: 120 us -> 0.58 us  [local(): jnp.stack([lax.axis_index('env'), lax.axis_index('pts')]).astype(jnp.int32)]
    all_gather x4 -> x0, blocking collectives: 98.2 us -> none  [the longest x1 34.4 us: local(): lax.all_gather(gram_block[:, :col_block], PTS, axis=1, tiled=True)]
    all_to_all x1 -> x0, waiting for transfers between devices: 33.3 us -> none  [summed_on_arrival(): lax.all_to_all(cut_along(shard, dim, count), axis, 0, 0, tiled=True)]
    another operation x20 -> x0, local copies, waits for them, and re-layouts: 17.3 us -> none  [the longest x13 11.5 us: local(): jax.scipy.linalg.solve_triangular(low_factor, panel_rows.T, lower=True)]
    dot_general x3 -> x0, matrix products: 14.7 us -> none  [the longest x1 10.6 us: local(): lax.dot_general(lax.all_gather(own_tile, PTS, axis=1, tiled=True), weight...]
    another operation x20 -> x0, matrix products: 8.42 us -> none  [the longest x7 4.68 us: local(): jax.scipy.linalg.solve_triangular(low_factor, top_rows, lower=True)]
  transfers between devices with their start and end apart: 4 -> 0, of which waited for: 4 -> 0; matrix products, arithmetic and copies ran while one was open for 0% -> 0% of each run, Pallas kernels for 0% -> 0%
where the time goes in v2:
time: 162 us
  Pallas kernels  151 us (93%)
  local copies, waits for them, and re-layouts  9.09 us (6%)
    pallas_call x1, Pallas kernels, kernel_gram(): pl.pallas_call(gather_and_multiply, out_shape=(jax.ShapeDtypeStruct((5, 2...  71.6 us
    pallas_call x1, Pallas kernels, share(): pl.pallas_call(reduce_and_share, out_shape=(jax.ShapeDtypeStruct((16, 32,...  57.4 us
    pallas_call x1, Pallas kernels, factor(): pl.pallas_call(factor_and_update, out_shape=(jax.ShapeDtypeStruct((160, 3...  22.2 us
    unnamed x15, local copies, waits for them, and re-layouts  6.89 us

profile of v2, /device:TPU:1, one launch (start us, length us, event | category | flops | bytes accessed | tf_op | source)
XLA Modules:
  0.0 161.5 jit_solution(7302814497950057551)
XLA Ops:
  0.6 0.0 copy-start.6
  0.6 1.6 copy.5.points
  2.2 0.0 copy-done.6
  2.2 0.6 broadcast_in_dim.2.weight
  2.8 71.6 %shard_map.50 = (f32[5,256,128]{2,1,0:T(8,128)}, f32[16,32,256]{2,1,0:T(8,128)}) custom-call(f32[64,1024]{1,0:T(8,128)} %desc.1, f32[160,64]{1,0:T(8,128)} %copy.5.points, f32[8,1024]{1,0:T(8,128)} %broadcast_in_dim.2.weight), custom_call_target="tpu_custom_call" | custom-call | tf_op jit(solution)/shard_map/pallas_call | solution.py:280
  74.4 0.0 copy-start.1
  74.4 1.1 copy-done.1
  75.5 0.0 copy-start.4
  75.5 1.0 copy-done.4
  76.6 57.4 %shard_map.51 = (f32[16,32,512]{2,1,0:T(8,128)S(1)}, f32[16,32,256]{2,1,0:T(8,128)S(1)}, f32[16,32,256]{2,1,0:T(8,128)S(1)}, f32[128,128]{1,0:T(8,128)S(1)}) custom-call(f32[5,256,128]{2,1,0:T(8,128)S(1)} %copy-done.1, f32[16,32,256]{2,1,0:T(8,128)S(1)} %copy-done.4), custom_call_target="tpu_custom_call" | custom-call | tf_op jit(solution)/shard_map/pallas_call | solution.py:436
  133.9 0.0 copy-start
  133.9 1.0 copy-done
  134.9 0.0 copy-start.2
  134.9 0.8 copy-done.2
  135.7 0.0 copy-start.3
  135.7 0.8 copy-done.3
  136.5 0.0 copy-start.5
  136.5 0.6 copy-done.5
  137.1 0.6 pad_add_fusion.where
  137.7 22.2 %shard_map.52 = (f32[160,32]{1,0:T(8,128)}, f32[128,128]{1,0:T(8,128)}) custom-call(s32[2]{0:T(128)} %pad_add_fusion.where, f32[16,32,512]{2,1,0:T(8,128)} %copy-done, f32[16,32,256]{2,1,0:T(8,128)} %copy-done.2, f32[16,32,256]{2,1,0:T(8,128)} %copy-done.3, f32[128,128]{1,0:T(8,128)} %copy-done.5), custom_call_target="tpu_custom_call" | custom-call | tf_op jit(solution)/shard_map/pallas_call | solution.py:536
  159.9 1.6 copy.6
Async XLA Ops:
  0.6 1.6 copy-start.6
  74.4 1.1 copy-start.1
  75.5 1.0 copy-start.4
  133.9 1.0 copy-start
  134.9 0.8 copy-start.2
  135.7 0.8 copy-start.3
  136.5 0.6 copy-start.5

commit v3 on v2

--- a/solution.py
+++ b/solution.py
@@ -48,7 +48,7 @@
 
 
 def gather_and_multiply(
-    desc, points, weight, tt_out, panel_out,
+    desc, points, weight, tt_out, panel_out, corner_out,
     half, other_weight, line, table, feats, feats_hi, feats_lo, rows_hi, rows_lo, kp, kt,
     half_s, half_r, swap_s, swap_r, local_s, zp_s, zp_r, zt_s, zt_r, slab_s, slab_r, slabx_s, slabx_r,
     ring_s, ring_r, ringx_s, ringx_r,
@@ -266,9 +266,8 @@
 
     def panel(i, carry):
         a = halves(kp[pl.ds(pl.multiple_of(128 * i, 128), 128)])
-        panel_out[pl.ds(4 * i, 4), :, 0:128] = dot3(a, trail, nt).reshape(4, 32, 128)
-        corner = jnp.concatenate([dot3(a, lead, nt), jnp.zeros((128, 96), F32)], axis=1)
-        panel_out[pl.ds(4 * i, 4), :, 128:256] = corner.reshape(4, 32, 128)
+        panel_out[pl.ds(4 * i, 4)] = dot3(a, trail, nt).reshape(4, 32, 128)
+        corner_out[i] = dot3(lead, a, nt)
         return carry
 
     lax.fori_loop(0, 4, panel, 0)
@@ -279,9 +278,13 @@
     vmem = pl.BlockSpec(memory_space=pltpu.VMEM)
     return pl.pallas_call(
         gather_and_multiply,
-        out_shape=(jax.ShapeDtypeStruct((5, 256, 128), F32), jax.ShapeDtypeStruct((16, 32, 256), F32)),
+        out_shape=(
+            jax.ShapeDtypeStruct((5, 256, 128), F32),
+            jax.ShapeDtypeStruct((16, 32, 128), F32),
+            jax.ShapeDtypeStruct((4, 32, 128), F32),
+        ),
         in_specs=[vmem] * 3,
-        out_specs=[vmem] * 2,
+        out_specs=[vmem] * 3,
         scratch_shapes=[
             pltpu.VMEM((80, 64), F32),
             pltpu.VMEM((8, 1024), F32),
@@ -301,158 +304,6 @@
         ],
         compiler_params=pltpu.CompilerParams(collective_id=0, has_side_effects=True, vmem_limit_bytes=60 * 2**20),
     )(desc, points, weight)
-
-
-def reduce_and_share(
-    tt, pp, corner, p_rows, p_cols, block,
-    p_in, tt_in, t_own, c_own, tt_own,
-    p_s, p_r, tt_s, tt_r, col_s, col_r, row_s, row_r, cor_s, cor_r, blk_s, blk_r,
-):
-    e, p, x, y, z, c = placed()
-    h = p // 8
-    me = 4 * x + y
-    barrier = pltpu.get_barrier_semaphore()
-
-    def is_me(to):
-        return (to[0] == e) & (to[1] == p)
-
-    def greet(who):
-        @pl.when(jnp.logical_not(is_me(who)))
-        def _():
-            pl.semaphore_signal(barrier, inc=1, device_id=who, device_id_type=MESH)
-
-    def send(src, dst, send_sem, recv_sem, to, also=None):
-        here, there = is_me(to), jnp.logical_not(is_me(to))
-        if also is not None:
-            here, there = here & also, there & also
-
-        @pl.when(here)
-        def _():
-            pltpu.make_async_copy(src, dst, recv_sem).start()
-
-        @pl.when(there)
-        def _():
-            remote(src, dst, send_sem, recv_sem, to).start()
-
-        def finish():
-            @pl.when(there)
-            def _():
-                remote(src, dst, send_sem, recv_sem, to).wait_send()
-
-        return finish
-
-    z_row, z_col = e % 8, z
-    apart = (z_col + 8 - z_row) % 8
-    straight = apart <= 4
-    gap = jnp.where(straight, apart, 8 - apart)
-    z_first = jnp.where(straight, z_row, z_col)
-    h_first = jnp.where(straight, e // 8, h)
-    h_second = jnp.where(straight, h, e // 8)
-    z_from = (z_first + 8 - jnp.where(gap == 3, 1, 0)) % 8
-    c_from = jnp.where(gap == 0, h_second, jnp.where(gap >= 3, 1, 0))
-
-    for q in range(16):
-        greet(device(q // 4, q % 4, z, h))
-        greet(device(q // 4, q % 4, z, c))
-        greet((q, p))
-        greet((q, e))
-    for t in range(8):
-        q = 8 * h_first + t
-        greet(device(q // 4, q % 4, z_from, c_from))
-
-    owners = []
-    for k in range(5):
-        first = (k + 1) // 2
-        d_row = c if first == 1 else 0
-        d_col = (0, 1 + 3 * c, 2 + 2 * c)[first]
-        side = c if k == 0 else (k + 1) % 2
-        p_a = 8 * (me // 8) + (z + d_row) % 8
-        p_b = 8 * side + (z + d_col) % 8
-        owners.append((2 * k, k, (p_a, p_b), None))
-        if k > 0:
-            owners.append((2 * k + 1, k, (p_b, p_a), None if first == 1 else c == 0))
-
-    targets = [(a, 8 * c + z) for a in range(16)] + [device(q // 4, q % 4, z, c) for q in range(16)]
-    targets += [(p, q) for q in range(16)] + [(q, p) for q in range(16)]
-    expected = 0
-    for to in targets:
-        expected = expected + jnp.where(is_me(to), 0, 1)
-    for _, _, to, also in owners:
-        counts = jnp.logical_not(is_me(to)) if also is None else jnp.logical_not(is_me(to)) & also
-        expected = expected + jnp.where(counts, 1, 0)
-    pl.semaphore_wait(barrier, expected)
-
-    pending = []
-    for a in range(16):
-        pending.append(send(pp.at[a], p_in.at[me], p_s.at[a], p_r.at[me], (a, 8 * c + z)))
-    for q in range(16):
-        to = device(q // 4, q % 4, z, c)
-        pending.append(send(tt.at[:, 16 * q : 16 * q + 16], tt_in.at[me], tt_s.at[q], tt_r.at[me], to))
-
-    for q in range(16):
-        arrived(p_in.at[q], p_r.at[q])
-    total = p_in[0]
-    for q in range(1, 16):
-        total = total + p_in[q]
-    at = lax.broadcasted_iota(jnp.int32, (32, 256), 1)
-    one = (at == 128 + lax.broadcasted_iota(jnp.int32, (32, 256), 0)) & (e == p)
-    t_own[...] = total + jnp.where(one, 1.0, 0.0)
-    for q in range(16):
-        pending.append(send(t_own, p_rows.at[e], row_s.at[q], row_r.at[e], (p, q)))
-    for q in range(16):
-        pending.append(send(t_own, p_cols.at[e], col_s.at[q], col_r.at[e], (q, p)))
-
-    for q in range(16):
-        arrived(p_rows.at[q], row_r.at[q])
-    for q in range(4):
-        strip = p_rows[4 * q : 4 * q + 4, :, 128:256].reshape(128, 128)
-        c_own[:, 128 * q : 128 * q + 128] = jnp.transpose(strip)[0:32]
-    for q in range(16):
-        pending.append(send(c_own, corner.at[e], cor_s.at[q], cor_r.at[e], (q, p)))
-
-    for q in range(16):
-        arrived(tt_in.at[q], tt_r.at[q])
-    total = tt_in[0]
-    for q in range(1, 16):
-        total = total + tt_in[q]
-    tt_own[...] = total
-    part = me % 8
-    rows = pl.ds(pl.multiple_of(16 * part, 16), 16)
-    for n, k, to, also in owners:
-        pending.append(send(tt_own.at[k], block.at[rows], blk_s.at[n], blk_r.at[part], to, also))
-
-    for q in range(16):
-        arrived(p_cols.at[q], col_r.at[q])
-        arrived(corner.at[q], cor_r.at[q])
-    for t in range(8):
-        arrived(block.at[16 * t : 16 * t + 16], blk_r.at[t])
-    for finish in pending:
-        finish()
-
-
-def share(tt, pp):
-    dma = pltpu.SemaphoreType.DMA
-    vmem = pl.BlockSpec(memory_space=pltpu.VMEM)
-    return pl.pallas_call(
-        reduce_and_share,
-        out_shape=(
-            jax.ShapeDtypeStruct((16, 32, 512), F32),
-            jax.ShapeDtypeStruct((16, 32, 256), F32),
-            jax.ShapeDtypeStruct((16, 32, 256), F32),
-            jax.ShapeDtypeStruct((128, 128), F32),
-        ),
-        in_specs=[vmem] * 2,
-        out_specs=[vmem] * 4,
-        scratch_shapes=[
-            pltpu.VMEM((16, 32, 256), F32),
-            pltpu.VMEM((16, 5, 16, 128), F32),
-            pltpu.VMEM((32, 256), F32),
-            pltpu.VMEM((32, 512), F32),
-            pltpu.VMEM((5, 16, 128), F32),
-        ]
-        + [dma((16,))] * 12,
-        compiler_params=pltpu.CompilerParams(collective_id=1, has_side_effects=True, vmem_limit_bytes=32 * 2**20),
-    )(tt, pp)
 
 
 def dot_hi(a, b, dims):
@@ -501,59 +352,239 @@
             e_ref[8 * g : 8 * g + 8, :] = e
 
 
-def factor_and_update(where, corner, p_rows, p_cols, block, panel_ref, trail_ref, a, ui, uj, d, inv_ref):
-    e, p = where[0], where[1]
+def finish_panel(
+    tt, pp, cc, panel_ref, trail_ref,
+    c_in, c_z, c_all, p_in, p_rows, p_cols, t_own, tt_in, tt_own, block, a, ui, uj, d, inv_ref, strip,
+    c_s, c_r, cz_s, cz_r, cp_s, cp_r, cx_s, cx_r, keep_s,
+    p_s, p_r, tt_s, tt_r, col_s, col_r, row_s, row_r, blk_s, blk_r,
+):
+    e, p, x, y, z, c = placed()
+    h = p // 8
+    me = 4 * x + y
+    sibling = device(x, y, z, 1 - c)
+    in_plane = lambda q: device((x + q // 4) % 4, (y + q % 4) % 4, z, c)
+    index_at = lambda q: 4 * ((x + q // 4) % 4) + (y + q % 4) % 4
+    index_from = lambda q: 4 * ((x + 4 - q // 4) % 4) + (y + 4 - q % 4) % 4
+    along_z = lambda q: device(x, y, (z + q) % 8, c)
+    barrier = pltpu.get_barrier_semaphore()
+
+    def is_me(to):
+        return (to[0] == e) & (to[1] == p)
+
+    def greet(who):
+        @pl.when(jnp.logical_not(is_me(who)))
+        def _():
+            pl.semaphore_signal(barrier, inc=1, device_id=who, device_id_type=MESH)
+
+    def send(src, dst, send_sem, recv_sem, to, also=None):
+        here, there = is_me(to), jnp.logical_not(is_me(to))
+        if also is not None:
+            here, there = here & also, there & also
+
+        @pl.when(here)
+        def _():
+            pltpu.make_async_copy(src, dst, recv_sem).start()
+
+        @pl.when(there)
+        def _():
+            remote(src, dst, send_sem, recv_sem, to).start()
+
+        def finish():
+            @pl.when(there)
+            def _():
+                remote(src, dst, send_sem, recv_sem, to).wait_send()
+
+        return finish
+
+    z_row, z_col = e % 8, z
+    apart = (z_col + 8 - z_row) % 8
+    straight = apart <= 4
+    gap = jnp.where(straight, apart, 8 - apart)
+    z_first = jnp.where(straight, z_row, z_col)
+    h_first = jnp.where(straight, e // 8, h)
+    h_second = jnp.where(straight, h, e // 8)
+    z_from = (z_first + 8 - jnp.where(gap == 3, 1, 0)) % 8
+    c_from = jnp.where(gap == 0, h_second, jnp.where(gap >= 3, 1, 0))
+
+    owners = []
+    for k in range(5):
+        first = (k + 1) // 2
+        d_row = c if first == 1 else 0
+        d_col = (0, 1 + 3 * c, 2 + 2 * c)[first]
+        side = c if k == 0 else (k + 1) % 2
+        p_a = 8 * (me // 8) + (z + d_row) % 8
+        p_b = 8 * side + (z + d_col) % 8
+        owners.append((2 * k, k, (p_a, p_b), None))
+        if k > 0:
+            owners.append((2 * k + 1, k, (p_b, p_a), None if first == 1 else c == 0))
+
+    pl.semaphore_signal(barrier, inc=1, device_id=sibling, device_id_type=MESH)
+    for q in range(1, 16):
+        pl.semaphore_signal(barrier, inc=1, device_id=in_plane(q), device_id_type=MESH)
+    for q in range(1, 8):
+        pl.semaphore_signal(barrier, inc=1, device_id=along_z(q), device_id_type=MESH)
+    for q in range(16):
+        greet(device(q // 4, q % 4, z, h))
+        greet((q, p))
+        greet((q, e))
+    for t in range(8):
+        q = 8 * h_first + t
+        greet(device(q // 4, q % 4, z_from, c_from))
+    targets = [(q, 8 * c + z) for q in range(16)] + [(p, q) for q in range(16)] + [(q, p) for q in range(16)]
+    expected = 23
+    for to in targets:
+        expected = expected + jnp.where(is_me(to), 0, 1)
+    for _, _, to, also in owners:
+        counts = jnp.logical_not(is_me(to)) if also is None else jnp.logical_not(is_me(to)) & also
+        expected = expected + jnp.where(counts, 1, 0)
+    pl.semaphore_wait(barrier, expected)
+
+    pending, plain = [], []
+
+    def go(copy):
+        copy.start()
+        plain.append(copy)
+
+    def corner_rows(q):
+        return pl.ds(pl.multiple_of(8 * (q // 4), 8), 8)
+
+    stay = pltpu.make_async_copy(cc.at[me % 4, corner_rows(me)], c_in.at[me], c_r.at[0])
+    stay.start()
+    for q in range(1, 16):
+        there = index_at(q)
+        go(remote(cc.at[there % 4, corner_rows(there)], c_in.at[me], c_s.at[q], c_r.at[q], in_plane(q)))
+    for q in range(16):
+        pending.append(send(pp.at[q], p_in.at[me], p_s.at[q], p_r.at[me], (q, 8 * c + z)))
+
+    for q in range(16):
+        arrived(c_in.at[index_from(q)], c_r.at[q])
+    total = c_in[0]
+    for q in range(1, 16):
+        total = total + c_in[q]
+    at_row = 256 * c + 32 * z + 8 * (me // 4) + lax.broadcasted_iota(jnp.int32, (8, 128), 0)
+    at_col = 128 * (me % 4) + lax.broadcasted_iota(jnp.int32, (8, 128), 1)
+    c_z[z] = total + jnp.where(at_row == at_col, 1.0, 0.0)
+    for q in range(1, 8):
+        go(remote(c_z.at[z], c_z.at[z], cz_s.at[q], cz_r.at[q], along_z(q)))
+    for q in range(1, 8):
+        arrived(c_z.at[(z + 8 - q) % 8], cz_r.at[q])
+
+    def corner_part(q, core):
+        return c_all.at[core, :, q // 4, :, pl.ds(pl.multiple_of(128 * (q % 4), 128), 128)]
+
+    for q in range(1, 16):
+        go(remote(c_z, corner_part(me, c), cp_s.at[q], cp_r.at[q], in_plane(q)))
+    go(remote(c_z, corner_part(me, c), cx_s.at[0], cx_r.at[0], sibling))
+    keep = pltpu.make_async_copy(c_z, corner_part(me, c), keep_s)
+    keep.start()
+
+    for q in range(16):
+        arrived(p_in.at[q], p_r.at[q])
+    total = p_in[0]
+    for q in range(1, 16):
+        total = total + p_in[q]
+    t_own[...] = total
+    for q in range(16):
+        pending.append(send(t_own, p_rows.at[e], row_s.at[q], row_r.at[e], (p, q)))
+        pending.append(send(t_own, p_cols.at[e], col_s.at[q], col_r.at[e], (q, p)))
+
+    for q in range(1, 16):
+        part = corner_part(index_from(q), c)
+        arrived(part, cp_r.at[q])
+        go(remote(part, part, cx_s.at[q], cx_r.at[q], sibling))
+    for q in range(16):
+        go_to = device(q // 4, q % 4, z, c)
+        pending.append(send(tt.at[:, 16 * q : 16 * q + 16], tt_in.at[me], tt_s.at[q], tt_r.at[me], go_to))
+    keep.wait()
+    for q in range(16):
+        arrived(corner_part(index_from(q), 1 - c), cx_r.at[q])
+
     n = a.shape[0]
-    a[...] = corner[...].reshape(n, n)
-    ui[...] = p_rows[...].reshape(n, 256)
-    uj[...] = p_cols[:, :, 0:128].reshape(n, 128)
+    a[...] = c_all[...].reshape(n, n)
+    ui[:, 128:256] = a[:, pl.ds(pl.multiple_of(128 * (e // 4), 128), 128)]
     for k in range(n // NB):
         lo, hi = k * NB, (k + 1) * NB
         d[...] = a[lo:hi, lo:hi]
         inverse_factor(d, inv_ref)
         inv = inv_ref[...]
-        ui[lo:hi, :] = dot_hi(inv, ui[lo:hi, :], ((1,), (0,)))
-        uj[lo:hi, :] = dot_hi(inv, uj[lo:hi, :], ((1,), (0,)))
         if hi < n:
             a[lo:hi, hi:] = dot_hi(inv, a[lo:hi, hi:], ((1,), (0,)))
             u = a[lo:hi, hi:]
             a[hi:, hi:] -= dot_hi(u, u, ((0,), (0,)))
+        if k == 0:
+            for q in range(16):
+                arrived(tt_in.at[q], tt_r.at[q])
+            total = tt_in[0]
+            for q in range(1, 16):
+                total = total + tt_in[q]
+            tt_own[...] = total
+            part = me % 8
+            rows = pl.ds(pl.multiple_of(16 * part, 16), 16)
+            for m, kk, to, also in owners:
+                pending.append(send(tt_own.at[kk], block.at[rows], blk_s.at[m], blk_r.at[part], to, also))
+            for q in range(16):
+                arrived(p_rows.at[q], row_r.at[q])
+                arrived(p_cols.at[q], col_r.at[q])
+            ui[:, 0:128] = p_rows[...].reshape(n, 128)
+            uj[...] = p_cols[...].reshape(n, 128)
+        ui[lo:hi, :] = dot_hi(inv, ui[lo:hi, :], ((1,), (0,)))
+        uj[lo:hi, :] = dot_hi(inv, uj[lo:hi, :], ((1,), (0,)))
+        if hi < n:
             ui[hi:, :] -= dot_hi(u, ui[lo:hi, :], ((0,), (0,)))
             uj[hi:, :] -= dot_hi(u, uj[lo:hi, :], ((0,), (0,)))
+    for t in range(8):
+        arrived(block.at[16 * t : 16 * t + 16], blk_r.at[t])
     gram = block[...]
-    straight = (p % 8 + 8 - e % 8) % 8 <= 4
     gram = jnp.where(straight, gram, jnp.transpose(gram))
     same = lax.broadcasted_iota(jnp.int32, (128, 128), 0) == lax.broadcasted_iota(jnp.int32, (128, 128), 1)
     gram = gram + jnp.where(same & (e == p), 1.0, 0.0)
     trail_ref[...] = gram - dot_hi(ui[:, 0:128], uj[...], ((0,), (0,)))
-    strip = jnp.transpose(ui[pl.ds(pl.multiple_of(32 * p, 32), 32), :])
-    panel_ref[0:32, :] = strip[128:160]
-    panel_ref[32:160, :] = strip[0:128]
-
-
-def factor(where, corner, p_rows, p_cols, block):
+    across = jnp.transpose(ui[pl.ds(pl.multiple_of(32 * p, 32), 32), :])
+    strip[...] = across[128:256]
+    panel_ref[0:32, :] = strip[pl.ds(pl.multiple_of(32 * (e % 4), 32), 32), :]
+    panel_ref[32:160, :] = across[0:128]
+    for copy in plain:
+        copy.wait_send()
+    for finish in pending:
+        finish()
+
+
+def finish(tt, pp, cc):
+    dma = pltpu.SemaphoreType.DMA
     vmem = pl.BlockSpec(memory_space=pltpu.VMEM)
     return pl.pallas_call(
-        factor_and_update,
+        finish_panel,
         out_shape=(jax.ShapeDtypeStruct((160, 32), F32), jax.ShapeDtypeStruct((128, 128), F32)),
-        in_specs=[pl.BlockSpec(memory_space=pltpu.SMEM)] + [vmem] * 4,
+        in_specs=[vmem] * 3,
         out_specs=[vmem] * 2,
         scratch_shapes=[
+            pltpu.VMEM((16, 8, 128), F32),
+            pltpu.VMEM((8, 8, 128), F32),
+            pltpu.VMEM((2, 8, 4, 8, 512), F32),
+            pltpu.VMEM((16, 32, 128), F32),
+            pltpu.VMEM((16, 32, 128), F32),
+            pltpu.VMEM((16, 32, 128), F32),
+            pltpu.VMEM((32, 128), F32),
+            pltpu.VMEM((16, 5, 16, 128), F32),
+            pltpu.VMEM((5, 16, 128), F32),
+            pltpu.VMEM((128, 128), F32),
             pltpu.VMEM((512, 512), F32),
             pltpu.VMEM((512, 256), F32),
             pltpu.VMEM((512, 128), F32),
             pltpu.VMEM((NB, NB), F32),
             pltpu.VMEM((NB, NB), F32),
-        ],
-    )(where, corner, p_rows, p_cols, block)
+            pltpu.VMEM((128, 32), F32),
+        ]
+        + [dma((16,))] * 8
+        + [dma]
+        + [dma((16,))] * 10,
+        compiler_params=pltpu.CompilerParams(collective_id=1, has_side_effects=True, vmem_limit_bytes=32 * 2**20),
+    )(tt, pp, cc)
 
 
 def local(descriptors, env_weight, points):
     weight = jnp.broadcast_to(env_weight[None, :], (8, env_weight.shape[0]))
-    tt, pp = kernel_gram(descriptors, points, weight)
-    shared = share(tt, pp)
-    where = jnp.stack([lax.axis_index("env"), lax.axis_index("pts")]).astype(jnp.int32)
-    return factor(where, *shared)
+    return finish(*kernel_gram(descriptors, points, weight))
 
 
 def solution(mesh):

time: 162 us -> 139 us (0.86)
  Pallas kernels: 151 us -> 131 us
  local copies, waits for them, and re-layouts: 9.09 us -> 7.06 us
    pallas_call x2 -> x1, Pallas kernels: 79.6 us -> 59.5 us  [finish(): pl.pallas_call(finish_panel, out_shape=(jax.ShapeDtypeStruct((160, 32), F...]
    unnamed x15 -> x8, local copies, waits for them, and re-layouts: 6.89 us -> 5.07 us
where the time goes in v3:
time: 139 us
  Pallas kernels  131 us (94%)
  local copies, waits for them, and re-layouts  7.06 us (5%)
    pallas_call x1, Pallas kernels, kernel_gram(): pl.pallas_call(gather_and_multiply, out_shape=(jax.ShapeDtypeStruct((5, 2...  71.5 us
    pallas_call x1, Pallas kernels, finish(): pl.pallas_call(finish_panel, out_shape=(jax.ShapeDtypeStruct((160, 32), F...  59.5 us
    unnamed x8, local copies, waits for them, and re-layouts  5.07 us

profile of v3, /device:TPU:1, one launch (start us, length us, event | category | flops | bytes accessed | tf_op | source)
XLA Modules:
  0.0 138.7 jit_solution(5201658185786116507)
XLA Ops:
  0.6 1.3 broadcast_in_dim.2.weight
  1.9 1.6 %copy.5.points = f32[160,64]{1,0:T(8,128)} copy(f32[160,64]{0,1:T(8,128)} %param.5) | data formatting | bytes 81920 | tf_op args[2]
  3.5 71.5 %shard_map.50 = (f32[5,256,128]{2,1,0:T(8,128)}, f32[16,32,128]{2,1,0:T(8,128)}, f32[4,32,128]{2,1,0:T(8,128)}) custom-call(f32[64,1024]{1,0:T(8,128)} %desc.1, f32[160,64]{1,0:T(8,128)} %copy.5.points, f32[8,1024]{1,0:T(8,128)} %broadcast_in_dim.2.weight), custom_call_target="tpu_custom_call" | custom-call | tf_op jit(solution)/shard_map/pallas_call | solution.py:279
  75.0 0.0 copy-start
  75.0 1.1 copy-done
  76.1 0.0 copy-start.1
  76.1 0.9 copy-done.1
  77.0 0.0 copy-start.2
  77.0 0.8 copy-done.2
  77.9 59.5 %shard_map.51 = (f32[160,32]{1,0:T(8,128)S(1)}, f32[128,128]{1,0:T(8,128)S(1)}) custom-call(f32[5,256,128]{2,1,0:T(8,128)S(1)} %copy-done, f32[16,32,128]{2,1,0:T(8,128)S(1)} %copy-done.1, f32[4,32,128]{2,1,0:T(8,128)S(1)} %copy-done.2), custom_call_target="tpu_custom_call" | custom-call | tf_op jit(solution)/shard_map/pallas_call | solution.py:555
  137.3 0.7 copy.6
  138.0 0.6 copy.8
Async XLA Ops:
  75.0 1.1 copy-start
  76.1 0.9 copy-start.1
  77.0 0.8 copy-start.2

commit v4 on v3

--- a/solution.py
+++ b/solution.py
@@ -47,13 +47,13 @@
     return one(a[0], b[0]) + (one(a[0], b[1]) + one(a[1], b[0]))
 
 
-def gather_and_multiply(
-    desc, points, weight, tt_out, panel_out, corner_out,
-    half, other_weight, line, table, feats, feats_hi, feats_lo, rows_hi, rows_lo, kp, kt,
+def gather(
+    spots, desc, points, weight,
+    half, other_weight, line, table, feats,
     half_s, half_r, swap_s, swap_r, local_s, zp_s, zp_r, zt_s, zt_r, slab_s, slab_r, slabx_s, slabx_r,
     ring_s, ring_r, ringx_s, ringx_r,
 ):
-    e, p, x, y, z, c = placed()
+    e, p, x, y, z, c = spots
     h = p // 8
     native = c == h
     turn = jnp.where(native, 1, 7)
@@ -69,13 +69,6 @@
         sy = (y + 8 - j1 * core - j2 * (1 - core)) % 4
         lanes = pl.multiple_of(128 * (2 * sx + sy % 2), 128)
         return table.at[sy // 2, core, :, pl.ds(lanes, 128)]
-
-    barrier = pltpu.get_barrier_semaphore()
-    greet = [sibling, partner] + [along_z(d) for d in range(1, 8)]
-    greet += [device(*step(j, 0), z, c) for j in (1, 2, 3)] + [device(*step(0, j), z, c) for j in (1, 2, 3)]
-    for who in greet:
-        pl.semaphore_signal(barrier, inc=1, device_id=who, device_id_type=MESH)
-    pl.semaphore_wait(barrier, len(greet))
 
     o = 1 - c
     to_sibling = [
@@ -85,16 +78,19 @@
     ]
     for copy in to_sibling:
         copy.start()
-    swap = remote(desc, feats.at[p], swap_s, swap_r, partner)
-    keep = pltpu.make_async_copy(desc, feats.at[p], swap_r)
+    parts = [pl.ds(32 * n, 32) for n in range(2)]
+    swap = [remote(desc.at[r], feats.at[p, r], swap_s.at[n], swap_r.at[n], partner) for n, r in enumerate(parts)]
+    keep = [pltpu.make_async_copy(desc.at[r], feats.at[p, r], swap_r.at[n]) for n, r in enumerate(parts)]
 
     @pl.when(native)
     def _():
-        keep.start()
+        for copy in keep:
+            copy.start()
 
     @pl.when(jnp.logical_not(native))
     def _():
-        swap.start()
+        for copy in swap:
+            copy.start()
 
     arrived(half.at[0:16], half_r.at[0])
     arrived(half.at[16:80], half_r.at[1])
@@ -116,29 +112,29 @@
     for copy in lined:
         copy.start()
 
-    def piece(m, core, sign):
+    def piece(m, n, core, sign):
         d = (0, 1, 2, 3, 4, 7, 6, 5)[m]
-        return feats.at[8 * core + (z + 8 * 8 - sign * d) % 8]
+        return feats.at[8 * core + (z + 8 * 8 - sign * d) % 8, parts[n]]
 
     rings, across = [], []
 
-    def pass_on(m):
-        src = piece(m, c, turn)
+    def pass_on(m, n):
+        src = piece(m, n, c, turn)
         if m in (0, 1, 2, 3):
-            copy = remote(src, src, ring_s.at[m + 1], ring_r.at[m + 1], along_z(turn))
-            copy.start()
-            rings.append(copy)
+            at = 2 * (m + 1) + n
+            rings.append(remote(src, src, ring_s.at[at], ring_r.at[at], along_z(turn)))
+            rings[-1].start()
         if m in (0, 5, 6):
-            n = 5 if m == 0 else m + 1
-            copy = remote(src, src, ring_s.at[n], ring_r.at[n], along_z(8 - turn))
-            copy.start()
-            rings.append(copy)
-        copy = remote(src, src, ringx_s.at[m], ringx_r.at[m], sibling)
-        copy.start()
-        across.append(copy)
-
-    arrived(piece(0, c, turn), swap_r)
-    pass_on(0)
+            at = 2 * (5 if m == 0 else m + 1) + n
+            rings.append(remote(src, src, ring_s.at[at], ring_r.at[at], along_z(8 - turn)))
+            rings[-1].start()
+        at = 2 * m + n
+        across.append(remote(src, src, ringx_s.at[at], ringx_r.at[at], sibling))
+        across[-1].start()
+
+    for n in range(2):
+        arrived(piece(0, n, c, turn), swap_r.at[n])
+        pass_on(0, n)
 
     for s in (1, 2, 3):
         arrived(line.at[pl.ds(128 + 64 * s, 64)], zt_r.at[s])
@@ -148,69 +144,89 @@
 
     slabs = []
 
-    def spread(j1, src, dst):
-        if j1 == 0:
-            for j in (1, 2, 3):
-                slabs.append(remote(src, dst, slab_s.at[4 * j], slab_r.at[4 * j], device(*step(j, 0), z, c)))
-                slabs[-1].start()
-        for j in (1, 2, 3):
-            n = 4 * j1 + j
-            slabs.append(remote(src, dst, slab_s.at[n], slab_r.at[n], device(*step(0, j), z, c)))
-            slabs[-1].start()
+    def forward(src, dst, j1, j2, to):
+        n = 4 * j1 + j2
+        slabs.append(remote(src, dst, slab_s.at[n], slab_r.at[n], device(*to, z, c)))
+        slabs[-1].start()
 
     def to_other_core(n, src, dst):
         slabs.append(remote(src, dst, slabx_s.at[n], slabx_r.at[n], sibling))
         slabs[-1].start()
 
     own = slab_of(0, 0, c)
-    spread(0, line, own)
+    forward(line, own, 1, 0, step(1, 0))
+    forward(line, own, 3, 0, step(3, 0))
+    forward(line, own, 0, 1, step(0, 1))
+    forward(line, own, 0, 3, step(0, 3))
     to_other_core(0, line, own)
     stay = pltpu.make_async_copy(line, own, local_s)
     stay.start()
 
     def take_piece(m):
-        arrived(piece(m, c, turn), ring_r.at[m])
-        pass_on(m)
+        for n in range(2):
+            arrived(piece(m, n, c, turn), ring_r.at[2 * m + n])
+            pass_on(m, n)
 
     def take_slab(j1, j2):
         here = slab_of(j1, j2, c)
         arrived(here, slab_r.at[4 * j1 + j2])
         if j2 == 0:
-            spread(j1, here, here)
+            if j1 == 1:
+                forward(here, here, 2, 0, step(1, 0))
+            forward(here, here, j1, 1, step(0, 1))
+            forward(here, here, j1, 3, step(0, 3))
+        if j2 == 1 and j1 in (0, 1):
+            forward(here, here, j1, 2, step(0, 1))
+        if j2 == 3 and j1 in (2, 3):
+            forward(here, here, j1, 2, step(0, 3))
         to_other_core(4 * j1 + j2, here, here)
 
     take_slab(1, 0)
     take_slab(3, 0)
     take_piece(1)
     take_piece(5)
-    take_slab(2, 0)
     take_slab(0, 1)
     take_slab(0, 3)
-    take_slab(0, 2)
+    take_slab(2, 0)
+    take_slab(1, 1)
+    take_slab(3, 3)
     take_piece(2)
     take_piece(6)
-    for j1 in (1, 3):
-        for j2 in (1, 3, 2):
-            take_slab(j1, j2)
+    take_slab(1, 3)
+    take_slab(3, 1)
+    take_slab(2, 3)
+    take_slab(2, 1)
+    take_slab(0, 2)
     take_piece(3)
     take_piece(7)
-    for j2 in (1, 3, 2):
-        take_slab(2, j2)
+    take_slab(1, 2)
+    take_slab(3, 2)
+    take_slab(2, 2)
     take_piece(4)
 
     for m in range(8):
-        arrived(piece(m, o, 8 - turn), ringx_r.at[m])
+        for n in range(2):
+            arrived(piece(m, n, o, 8 - turn), ringx_r.at[2 * m + n])
     for j1 in range(4):
         for j2 in range(4):
             arrived(slab_of(j1, j2, o), slabx_r.at[4 * j1 + j2])
     stay.wait()
     arrived(other_weight, half_r.at[2])
-    for copy in to_sibling + lined + rings + across + slabs:
-        copy.wait_send()
-
-    @pl.when(jnp.logical_not(native))
-    def _():
-        swap.wait_send()
+
+    def drain():
+        for copy in to_sibling + lined + rings + across + slabs:
+            copy.wait_send()
+
+        @pl.when(jnp.logical_not(native))
+        def _():
+            for copy in swap:
+                copy.wait_send()
+
+    return drain
+
+
+def kernel_values(spots, table, feats, feats_hi, feats_lo, rows_hi, rows_lo, kp, kt):
+    c = spots[-1]
 
     def split_feats(i, carry):
         hi, lo = halves(feats[i])
@@ -247,6 +263,10 @@
 
     lax.fori_loop(0, 4, kernel_rows, 0)
 
+
+def multiply(spots, weight, other_weight, kp, kt, tt_out, panel_out, corner_out, send_corner, send_panel):
+    e, p, x, y, z, c = spots
+    native = c == p // 8
     w = jnp.where(native, weight[0:1], other_weight[0:1]) * (1.0 / NENV)
     nt = ((1,), (1,))
 
@@ -260,50 +280,20 @@
         tt_out[k] = dot3(a, b, nt)
         return carry
 
-    lax.fori_loop(0, 5, unit, 0)
     trail = halves(kt[0, pl.ds(pl.multiple_of(128 * c, 128), 128)] * w)
     lead = halves(kp[pl.ds(pl.multiple_of(256 * c + 32 * z, 32), 32)] * w)
 
     def panel(i, carry):
         a = halves(kp[pl.ds(pl.multiple_of(128 * i, 128), 128)])
+        corner_out[i] = dot3(lead, a, nt)
         panel_out[pl.ds(4 * i, 4)] = dot3(a, trail, nt).reshape(4, 32, 128)
-        corner_out[i] = dot3(lead, a, nt)
         return carry
 
     lax.fori_loop(0, 4, panel, 0)
-
-
-def kernel_gram(desc, points, weight):
-    dma = pltpu.SemaphoreType.DMA
-    vmem = pl.BlockSpec(memory_space=pltpu.VMEM)
-    return pl.pallas_call(
-        gather_and_multiply,
-        out_shape=(
-            jax.ShapeDtypeStruct((5, 256, 128), F32),
-            jax.ShapeDtypeStruct((16, 32, 128), F32),
-            jax.ShapeDtypeStruct((4, 32, 128), F32),
-        ),
-        in_specs=[vmem] * 3,
-        out_specs=[vmem] * 3,
-        scratch_shapes=[
-            pltpu.VMEM((80, 64), F32),
-            pltpu.VMEM((8, 1024), F32),
-            pltpu.VMEM((384, 128), F32),
-            pltpu.VMEM((2, 2, 384, 1024), F32),
-            pltpu.VMEM((16, 64, 1024), F32),
-            pltpu.VMEM((1024, 1024), BF16),
-            pltpu.VMEM((1024, 1024), BF16),
-            pltpu.VMEM((320, 1024), BF16),
-            pltpu.VMEM((320, 1024), BF16),
-            pltpu.VMEM((512, 1024), F32),
-            pltpu.VMEM((3, 256, 1024), F32),
-            dma((3,)), dma((3,)), dma, dma, dma,
-            dma((8,)), dma((8,)), dma((4,)), dma((4,)),
-            dma((16,)), dma((16,)), dma((16,)), dma((16,)),
-            dma((8,)), dma((8,)), dma((8,)), dma((8,)),
-        ],
-        compiler_params=pltpu.CompilerParams(collective_id=0, has_side_effects=True, vmem_limit_bytes=60 * 2**20),
-    )(desc, points, weight)
+    send_corner()
+    lax.fori_loop(0, 1, unit, 0)
+    send_panel()
+    lax.fori_loop(1, 5, unit, 0)
 
 
 def dot_hi(a, b, dims):
@@ -352,13 +342,17 @@
             e_ref[8 * g : 8 * g + 8, :] = e
 
 
-def finish_panel(
-    tt, pp, cc, panel_ref, trail_ref,
+def whole(
+    desc, points, weight, panel_ref, trail_ref,
+    half, other_weight, line, table, feats, feats_hi, feats_lo, rows_hi, rows_lo, kp, kt, tt, pp, cc,
     c_in, c_z, c_all, p_in, p_rows, p_cols, t_own, tt_in, tt_own, block, a, ui, uj, d, inv_ref, strip,
+    half_s, half_r, swap_s, swap_r, local_s, zp_s, zp_r, zt_s, zt_r, slab_s, slab_r, slabx_s, slabx_r,
+    ring_s, ring_r, ringx_s, ringx_r,
     c_s, c_r, cz_s, cz_r, cp_s, cp_r, cx_s, cx_r, keep_s,
     p_s, p_r, tt_s, tt_r, col_s, col_r, row_s, row_r, blk_s, blk_r,
 ):
-    e, p, x, y, z, c = placed()
+    spots = placed()
+    e, p, x, y, z, c = spots
     h = p // 8
     me = 4 * x + y
     sibling = device(x, y, z, 1 - c)
@@ -419,6 +413,7 @@
             owners.append((2 * k + 1, k, (p_b, p_a), None if first == 1 else c == 0))
 
     pl.semaphore_signal(barrier, inc=1, device_id=sibling, device_id_type=MESH)
+    pl.semaphore_signal(barrier, inc=1, device_id=device(x, (y + 2) % 4, z, 1 - c), device_id_type=MESH)
     for q in range(1, 16):
         pl.semaphore_signal(barrier, inc=1, device_id=in_plane(q), device_id_type=MESH)
     for q in range(1, 8):
@@ -431,7 +426,7 @@
         q = 8 * h_first + t
         greet(device(q // 4, q % 4, z_from, c_from))
     targets = [(q, 8 * c + z) for q in range(16)] + [(p, q) for q in range(16)] + [(q, p) for q in range(16)]
-    expected = 23
+    expected = 24
     for to in targets:
         expected = expected + jnp.where(is_me(to), 0, 1)
     for _, _, to, also in owners:
@@ -439,6 +434,12 @@
         expected = expected + jnp.where(counts, 1, 0)
     pl.semaphore_wait(barrier, expected)
 
+    drain = gather(
+        spots, desc, points, weight, half, other_weight, line, table, feats,
+        half_s, half_r, swap_s, swap_r, local_s, zp_s, zp_r, zt_s, zt_r, slab_s, slab_r, slabx_s, slabx_r,
+        ring_s, ring_r, ringx_s, ringx_r,
+    )
+    kernel_values(spots, table, feats, feats_hi, feats_lo, rows_hi, rows_lo, kp, kt)
     pending, plain = [], []
 
     def go(copy):
@@ -448,13 +449,18 @@
     def corner_rows(q):
         return pl.ds(pl.multiple_of(8 * (q // 4), 8), 8)
 
-    stay = pltpu.make_async_copy(cc.at[me % 4, corner_rows(me)], c_in.at[me], c_r.at[0])
-    stay.start()
-    for q in range(1, 16):
-        there = index_at(q)
-        go(remote(cc.at[there % 4, corner_rows(there)], c_in.at[me], c_s.at[q], c_r.at[q], in_plane(q)))
-    for q in range(16):
-        pending.append(send(pp.at[q], p_in.at[me], p_s.at[q], p_r.at[me], (q, 8 * c + z)))
+    def send_corner():
+        stay = pltpu.make_async_copy(cc.at[me % 4, corner_rows(me)], c_in.at[me], c_r.at[0])
+        stay.start()
+        for q in range(1, 16):
+            there = index_at(q)
+            go(remote(cc.at[there % 4, corner_rows(there)], c_in.at[me], c_s.at[q], c_r.at[q], in_plane(q)))
+
+    def send_panel():
+        for q in range(16):
+            pending.append(send(pp.at[q], p_in.at[me], p_s.at[q], p_r.at[me], (q, 8 * c + z)))
+
+    multiply(spots, weight, other_weight, kp, kt, tt, pp, cc, send_corner, send_panel)
 
     for q in range(16):
         arrived(c_in.at[index_from(q)], c_r.at[q])
@@ -547,44 +553,41 @@
         copy.wait_send()
     for finish in pending:
         finish()
-
-
-def finish(tt, pp, cc):
+    drain()
+
+
+def fit(desc, points, weight):
     dma = pltpu.SemaphoreType.DMA
     vmem = pl.BlockSpec(memory_space=pltpu.VMEM)
+    f32 = lambda *shape: pltpu.VMEM(shape, F32)
+    bf16 = lambda *shape: pltpu.VMEM(shape, BF16)
     return pl.pallas_call(
-        finish_panel,
+        whole,
         out_shape=(jax.ShapeDtypeStruct((160, 32), F32), jax.ShapeDtypeStruct((128, 128), F32)),
         in_specs=[vmem] * 3,
         out_specs=[vmem] * 2,
         scratch_shapes=[
-            pltpu.VMEM((16, 8, 128), F32),
-            pltpu.VMEM((8, 8, 128), F32),
-            pltpu.VMEM((2, 8, 4, 8, 512), F32),
-            pltpu.VMEM((16, 32, 128), F32),
-            pltpu.VMEM((16, 32, 128), F32),
-            pltpu.VMEM((16, 32, 128), F32),
-            pltpu.VMEM((32, 128), F32),
-            pltpu.VMEM((16, 5, 16, 128), F32),
-            pltpu.VMEM((5, 16, 128), F32),
-            pltpu.VMEM((128, 128), F32),
-            pltpu.VMEM((512, 512), F32),
-            pltpu.VMEM((512, 256), F32),
-            pltpu.VMEM((512, 128), F32),
-            pltpu.VMEM((NB, NB), F32),
-            pltpu.VMEM((NB, NB), F32),
-            pltpu.VMEM((128, 32), F32),
+            f32(80, 64), f32(8, 1024), f32(384, 128), f32(2, 2, 384, 1024), f32(16, 64, 1024),
+            bf16(1024, 1024), bf16(1024, 1024), bf16(320, 1024), bf16(320, 1024),
+            f32(512, 1024), f32(3, 256, 1024), f32(5, 256, 128), f32(16, 32, 128), f32(4, 32, 128),
+            f32(16, 8, 128), f32(8, 8, 128), f32(2, 8, 4, 8, 512), f32(16, 32, 128), f32(16, 32, 128), f32(16, 32, 128),
+            f32(32, 128), f32(16, 5, 16, 128), f32(5, 16, 128), f32(128, 128),
+            f32(512, 512), f32(512, 256), f32(512, 128), f32(NB, NB), f32(NB, NB), f32(128, 32),
+            dma((3,)), dma((3,)), dma((2,)), dma((2,)), dma,
+            dma((8,)), dma((8,)), dma((4,)), dma((4,)),
+            dma((16,)), dma((16,)), dma((16,)), dma((16,)),
+            dma((16,)), dma((16,)), dma((16,)), dma((16,)),
         ]
         + [dma((16,))] * 8
         + [dma]
         + [dma((16,))] * 10,
-        compiler_params=pltpu.CompilerParams(collective_id=1, has_side_effects=True, vmem_limit_bytes=32 * 2**20),
-    )(tt, pp, cc)
+        compiler_params=pltpu.CompilerParams(collective_id=0, has_side_effects=True, vmem_limit_bytes=60 * 2**20),
+    )(desc, points, weight)
 
 
 def local(descriptors, env_weight, points):
     weight = jnp.broadcast_to(env_weight[None, :], (8, env_weight.shape[0]))
-    return finish(*kernel_gram(descriptors, points, weight))
+    return fit(descriptors, points, weight)
 
 
 def solution(mesh):

time: 139 us -> 122 us (0.88)
  Pallas kernels: 131 us -> 115 us
  local copies, waits for them, and re-layouts: 7.06 us -> 5.1 us
    pallas_call x2 -> x1, Pallas kernels: 131 us -> 115 us  [fit(): pl.pallas_call(whole, out_shape=(jax.ShapeDtypeStruct((160, 32), F32), ja...]
    unnamed x8 -> x4, local copies, waits for them, and re-layouts: 5.07 us -> 2.19 us
where the time goes in v4:
time: 122 us; the launch traced here: 121 us
  Pallas kernels  115 us (94%)
  local copies, waits for them, and re-layouts  5.1 us (4%)
    pallas_call x1, Pallas kernels, fit(): pl.pallas_call(whole, out_shape=(jax.ShapeDtypeStruct((160, 32), F32), ja...  115 us

profile of v4, /device:TPU:1, one launch (start us, length us, event | category | flops | bytes accessed | tf_op | source)
XLA Modules:
  0.0 120.9 jit_solution(8884918778467662798)
XLA Ops:
  0.6 1.3 %broadcast_in_dim.2.weight = f32[8,1024]{1,0:T(8,128)} broadcast(f32[1024]{0:T(1024)} %param.4), dimensions={1} | broadcast | bytes 36864 | tf_op jit(solution)/shard_map/broadcast_in_dim | solution.py:589
  1.9 1.6 %copy.5.points = f32[160,64]{1,0:T(8,128)} copy(f32[160,64]{0,1:T(8,128)} %param.5) | data formatting | bytes 81920 | tf_op args[2]
  3.5 115.2 %shard_map.50 = (f32[160,32]{1,0:T(8,128)}, f32[128,128]{1,0:T(8,128)}) custom-call(f32[64,1024]{1,0:T(8,128)} %desc.1, f32[160,64]{1,0:T(8,128)} %copy.5.points, f32[8,1024]{1,0:T(8,128)} %broadcast_in_dim.2.weight), custom_call_target="tpu_custom_call" | custom-call | tf_op jit(solution)/shard_map/pallas_call | solution.py:564
  118.7 0.0 copy-start
  118.7 1.6 %copy.6 = f32[160,32]{0,1:T(8,128)} copy(f32[160,32]{1,0:T(8,128)} %get-tuple-element.2) | data formatting | bytes 40960 | tf_op jit(solution)/shard_map/pallas_call | solution.py:564
  120.3 0.0 copy-done
  120.3 0.6 copy.8
Async XLA Ops:
  118.7 1.6 %copy-start = (f32[128,128]{1,0:T(8,128)S(1)}, f32[128,128]{1,0:T(8,128)}, u32[]{:S(2)}) copy-start(f32[128,128]{1,0:T(8,128)} %get-tuple-element.7) | copy-start | bytes 196612

commit v5 on v4

--- a/solution.py
+++ b/solution.py
@@ -49,8 +49,8 @@
 
 def gather(
     spots, desc, points, weight,
-    half, other_weight, line, table, feats,
-    half_s, half_r, swap_s, swap_r, local_s, zp_s, zp_r, zt_s, zt_r, slab_s, slab_r, slabx_s, slabx_r,
+    half, other_weight, line, table, extra, feats, feats_hi, feats_lo, rows_hi, rows_lo,
+    half_s, half_r, swap_s, swap_r, zp_s, zp_r, zt_s, zt_r, slab_s, slab_r, slabx_s, slabx_r,
     ring_s, ring_r, ringx_s, ringx_r,
 ):
     e, p, x, y, z, c = spots
@@ -68,7 +68,7 @@
         sx = (x + 8 - j1 * (1 - core) - j2 * core) % 4
         sy = (y + 8 - j1 * core - j2 * (1 - core)) % 4
         lanes = pl.multiple_of(128 * (2 * sx + sy % 2), 128)
-        return table.at[sy // 2, core, :, pl.ds(lanes, 128)]
+        return sy // 2, pl.ds(lanes, 128)
 
     o = 1 - c
     to_sibling = [
@@ -82,8 +82,25 @@
     swap = [remote(desc.at[r], feats.at[p, r], swap_s.at[n], swap_r.at[n], partner) for n, r in enumerate(parts)]
     keep = [pltpu.make_async_copy(desc.at[r], feats.at[p, r], swap_r.at[n]) for n, r in enumerate(parts)]
 
+    def piece(m, n, core, sign):
+        d = (0, 1, 2, 3, 4, 7, 6, 5)[m]
+        return feats.at[8 * core + (z + 8 * 8 - sign * d) % 8, parts[n]]
+
+    def first_sends(src, n):
+        dst = piece(0, n, c, turn)
+        return [
+            remote(src, dst, ring_s.at[2 + n], ring_r.at[2 + n], along_z(turn)),
+            remote(src, dst, ring_s.at[10 + n], ring_r.at[10 + n], along_z(8 - turn)),
+            remote(src, dst, ringx_s.at[n], ringx_r.at[n], sibling),
+        ]
+
+    first = [first_sends(piece(0, n, c, turn), n) for n in range(2)]
+
     @pl.when(native)
     def _():
+        for n in range(2):
+            for copy in first_sends(desc.at[parts[n]], n):
+                copy.start()
         for copy in keep:
             copy.start()
 
@@ -112,29 +129,28 @@
     for copy in lined:
         copy.start()
 
-    def piece(m, n, core, sign):
-        d = (0, 1, 2, 3, 4, 7, 6, 5)[m]
-        return feats.at[8 * core + (z + 8 * 8 - sign * d) % 8, parts[n]]
-
     rings, across = [], []
 
     def pass_on(m, n):
         src = piece(m, n, c, turn)
-        if m in (0, 1, 2, 3):
+        if m in (1, 2, 3):
             at = 2 * (m + 1) + n
             rings.append(remote(src, src, ring_s.at[at], ring_r.at[at], along_z(turn)))
             rings[-1].start()
-        if m in (0, 5, 6):
-            at = 2 * (5 if m == 0 else m + 1) + n
+        if m in (5, 6):
+            at = 2 * (m + 1) + n
             rings.append(remote(src, src, ring_s.at[at], ring_r.at[at], along_z(8 - turn)))
             rings[-1].start()
         at = 2 * m + n
         across.append(remote(src, src, ringx_s.at[at], ringx_r.at[at], sibling))
         across[-1].start()
 
-    for n in range(2):
-        arrived(piece(0, n, c, turn), swap_r.at[n])
-        pass_on(0, n)
+    @pl.when(jnp.logical_not(native))
+    def _():
+        for n in range(2):
+            arrived(piece(0, n, c, turn), swap_r.at[n])
+            for copy in first[n]:
+                copy.start()
 
     for s in (1, 2, 3):
         arrived(line.at[pl.ds(128 + 64 * s, 64)], zt_r.at[s])
@@ -149,26 +165,48 @@
         slabs.append(remote(src, dst, slab_s.at[n], slab_r.at[n], device(*to, z, c)))
         slabs[-1].start()
 
-    def to_other_core(n, src, dst):
-        slabs.append(remote(src, dst, slabx_s.at[n], slabx_r.at[n], sibling))
+    def third(core):
+        return pl.ds(pl.multiple_of(256 + 64 * core, 64), 64)
+
+    def to_other_core(n, src, at):
+        slabs.append(remote(src, extra.at[at[0], :, at[1]], slabx_s.at[n], slabx_r.at[n], sibling))
         slabs[-1].start()
 
-    own = slab_of(0, 0, c)
+    def split(value, rows, lanes):
+        hi, lo = halves(value)
+        rows_hi[rows, lanes] = hi
+        rows_lo[rows, lanes] = lo
+
+    def split_third(value, hh, cc, lanes):
+        split(value, pl.ds(pl.multiple_of(512 + 128 * hh + 64 * cc, 64), 64), lanes)
+
+    def split_piece(m, core, sign):
+        d = (0, 1, 2, 3, 4, 7, 6, 5)[m]
+        slot = 8 * core + (z + 8 * 8 - sign * d) % 8
+        hi, lo = halves(feats[slot])
+        at = pl.ds(pl.multiple_of(64 * slot, 64), 64)
+        feats_hi[at] = hi
+        feats_lo[at] = lo
+
+    mine_h, mine_lanes = slab_of(0, 0, c)
+    own = table.at[mine_h, :, mine_lanes]
     forward(line, own, 1, 0, step(1, 0))
     forward(line, own, 3, 0, step(3, 0))
     forward(line, own, 0, 1, step(0, 1))
     forward(line, own, 0, 3, step(0, 3))
-    to_other_core(0, line, own)
-    stay = pltpu.make_async_copy(line, own, local_s)
-    stay.start()
+    to_other_core(0, line.at[third(o)], (mine_h, mine_lanes))
+    split(line[0:256], pl.ds(pl.multiple_of(256 * mine_h, 256), 256), mine_lanes)
+    split_third(line[third(c)], mine_h, c, mine_lanes)
 
     def take_piece(m):
         for n in range(2):
             arrived(piece(m, n, c, turn), ring_r.at[2 * m + n])
             pass_on(m, n)
+        split_piece(m, c, turn)
 
     def take_slab(j1, j2):
-        here = slab_of(j1, j2, c)
+        hh, lanes = slab_of(j1, j2, c)
+        here = table.at[hh, :, lanes]
         arrived(here, slab_r.at[4 * j1 + j2])
         if j2 == 0:
             if j1 == 1:
@@ -179,7 +217,9 @@
             forward(here, here, j1, 2, step(0, 1))
         if j2 == 3 and j1 in (2, 3):
             forward(here, here, j1, 2, step(0, 3))
-        to_other_core(4 * j1 + j2, here, here)
+        to_other_core(4 * j1 + j2, table.at[hh, third(o), lanes], (hh, lanes))
+        split(table[hh, 0:256, lanes], pl.ds(pl.multiple_of(256 * hh, 256), 256), lanes)
+        split_third(table[hh, third(c), lanes], hh, c, lanes)
 
     take_slab(1, 0)
     take_slab(3, 0)
@@ -204,17 +244,25 @@
     take_slab(2, 2)
     take_piece(4)
 
-    for m in range(8):
+    @pl.when(native)
+    def _():
+        for n in range(2):
+            arrived(piece(0, n, c, turn), swap_r.at[n])
+
+    split_piece(0, c, turn)
+    for m in (0, 1, 5, 2, 6, 3, 7, 4):
         for n in range(2):
             arrived(piece(m, n, o, 8 - turn), ringx_r.at[2 * m + n])
+        split_piece(m, o, 8 - turn)
     for j1 in range(4):
         for j2 in range(4):
-            arrived(slab_of(j1, j2, o), slabx_r.at[4 * j1 + j2])
-    stay.wait()
+            hh, lanes = slab_of(j1, j2, o)
+            arrived(extra.at[hh, :, lanes], slabx_r.at[4 * j1 + j2])
+            split_third(extra[hh, :, lanes], hh, o, lanes)
     arrived(other_weight, half_r.at[2])
 
     def drain():
-        for copy in to_sibling + lined + rings + across + slabs:
+        for copy in to_sibling + lined + rings + across + slabs + first[0] + first[1]:
             copy.wait_send()
 
         @pl.when(jnp.logical_not(native))
@@ -225,46 +273,51 @@
     return drain
 
 
-def kernel_values(spots, table, feats, feats_hi, feats_lo, rows_hi, rows_lo, kp, kt):
-    c = spots[-1]
-
-    def split_feats(i, carry):
-        hi, lo = halves(feats[i])
-        rows = pl.ds(pl.multiple_of(64 * i, 64), 64)
-        feats_hi[rows] = hi
-        feats_lo[rows] = lo
-        return carry
-
-    lax.fori_loop(0, 16, split_feats, 0)
-
-    def kernel_rows(i, carry):
-        hh, cc = i // 2, i % 2
-        hi, lo = halves(table[hh, cc, 0:256])
-        rows_hi[0:256], rows_lo[0:256] = hi, lo
-        hi, lo = halves(table[hh, cc, pl.ds(pl.multiple_of(256 + 64 * c, 64), 64)])
-        rows_hi[256:320], rows_lo[256:320] = hi, lo
-
-        def columns(t, carry):
-            lanes = pl.ds(pl.multiple_of(256 * t, 256), 256)
-            scaled = dot3(
-                (rows_hi[...], rows_lo[...]), (feats_hi[:, lanes], feats_lo[:, lanes]), ((1,), (0,))
-            ) * (1.0 / 32.0)
-            value = 0.25 * scaled * scaled * scaled
-            for zz in range(8):
-                at = pl.multiple_of(256 * hh + 32 * zz + 16 * cc, 16)
-                kp[pl.ds(at, 16), lanes] = value[16 * zz : 16 * zz + 16]
-            for s in range(3):
-                at = pl.multiple_of(128 * hh + 64 * cc, 64)
-                kt[s, pl.ds(at, 64), lanes] = value[128 + 64 * s : 192 + 64 * s]
-            return carry
-
-        lax.fori_loop(0, 4, columns, 0)
-        return carry
-
-    lax.fori_loop(0, 4, kernel_rows, 0)
-
-
-def multiply(spots, weight, other_weight, kp, kt, tt_out, panel_out, corner_out, send_corner, send_panel):
+def kernel_values(spots, feats_hi, feats_lo, rows_hi, rows_lo, kp, kt, kp_s, kp_r, kt_s, kt_r):
+    e, p, x, y, z, c = spots
+    sibling = device(x, y, z, 1 - c)
+
+    def values(rows, lanes):
+        scaled = dot3((rows_hi[rows], rows_lo[rows]), (feats_hi[:, lanes], feats_lo[:, lanes]), ((1,), (0,))) * (1.0 / 32.0)
+        return 0.25 * scaled * scaled * scaled
+
+    sent = []
+
+    def exchange(t):
+        lanes = pl.ds(256 * t, 256)
+        lead, trail = kp.at[:, :, c, :, lanes], kt.at[0:2, :, c, :, lanes]
+        sent.append(remote(lead, lead, kp_s.at[t], kp_r.at[t], sibling))
+        sent.append(remote(trail, trail, kt_s.at[t], kt_r.at[t], sibling))
+        sent[-2].start()
+        sent[-1].start()
+
+    for t in range(4):
+        lanes = pl.ds(256 * t, 256)
+        value = values(pl.ds(0, 512), lanes)
+        for hh in range(2):
+            kp[hh, :, c, :, lanes] = value[256 * hh : 256 * hh + 128].reshape(8, 16, 256)
+            kt[0:2, hh, c, :, lanes] = value[256 * hh + 128 : 256 * hh + 256].reshape(2, 64, 256)
+        if t > 0:
+            exchange(t - 1)
+    for t in range(2):
+        lanes = pl.ds(512 * t, 512)
+        value = values(pl.ds(512, 256), lanes)
+        kt[2, :, :, :, lanes] = value.reshape(2, 2, 64, 512)
+        if t == 0:
+            exchange(3)
+    for t in range(4):
+        lanes = pl.ds(256 * t, 256)
+        arrived(kp.at[:, :, 1 - c, :, lanes], kp_r.at[t])
+        arrived(kt.at[0:2, :, 1 - c, :, lanes], kt_r.at[t])
+
+    def drain():
+        for copy in sent:
+            copy.wait_send()
+
+    return drain
+
+
+def multiply(spots, weight, other_weight, kp, kt, tt_out, panel_out, corner_out, send_corner):
     e, p, x, y, z, c = spots
     native = c == p // 8
     w = jnp.where(native, weight[0:1], other_weight[0:1]) * (1.0 / NENV)
@@ -275,25 +328,23 @@
         row = jnp.where(first == 1, c, 0)
         col = jnp.where(first == 0, 0, jnp.where(first == 1, 1 + c, 2))
         side = jnp.where(first == 0, c, (k + 1) % 2)
-        a = halves(kt[row] * w)
-        b = halves(kt[col, pl.ds(pl.multiple_of(128 * side, 128), 128)])
+        a = halves(kt[row].reshape(256, 1024) * w)
+        b = halves(kt[col, side].reshape(128, 1024))
         tt_out[k] = dot3(a, b, nt)
         return carry
 
-    trail = halves(kt[0, pl.ds(pl.multiple_of(128 * c, 128), 128)] * w)
-    lead = halves(kp[pl.ds(pl.multiple_of(256 * c + 32 * z, 32), 32)] * w)
+    trail = halves(kt[0, c].reshape(128, 1024) * w)
+    lead = halves(kp[c, z].reshape(32, 1024) * w)
 
     def panel(i, carry):
-        a = halves(kp[pl.ds(pl.multiple_of(128 * i, 128), 128)])
+        a = halves(kp[i // 2, pl.ds(4 * (i % 2), 4)].reshape(128, 1024))
         corner_out[i] = dot3(lead, a, nt)
         panel_out[pl.ds(4 * i, 4)] = dot3(a, trail, nt).reshape(4, 32, 128)
         return carry
 
     lax.fori_loop(0, 4, panel, 0)
     send_corner()
-    lax.fori_loop(0, 1, unit, 0)
-    send_panel()
-    lax.fori_loop(1, 5, unit, 0)
+    lax.fori_loop(0, 5, unit, 0)
 
 
 def dot_hi(a, b, dims):
@@ -343,11 +394,11 @@
 
 
 def whole(
-    desc, points, weight, panel_ref, trail_ref,
-    half, other_weight, line, table, feats, feats_hi, feats_lo, rows_hi, rows_lo, kp, kt, tt, pp, cc,
-    c_in, c_z, c_all, p_in, p_rows, p_cols, t_own, tt_in, tt_own, block, a, ui, uj, d, inv_ref, strip,
-    half_s, half_r, swap_s, swap_r, local_s, zp_s, zp_r, zt_s, zt_r, slab_s, slab_r, slabx_s, slabx_r,
-    ring_s, ring_r, ringx_s, ringx_r,
+    desc, points_t, weight, panel_ref, trail_ref,
+    points, half, other_weight, line, table, extra, feats, feats_hi, feats_lo, rows_hi, rows_lo, kp, kt, tt, pp, cc,
+    c_in, c_z, c_all, p_in, p_rows, p_cols, t_own, tt_in, tt_own, block, a, ui, uj, d, inv_ref,
+    half_s, half_r, swap_s, swap_r, zp_s, zp_r, zt_s, zt_r, slab_s, slab_r, slabx_s, slabx_r,
+    ring_s, ring_r, ringx_s, ringx_r, kp_s, kp_r, kt_s, kt_r,
     c_s, c_r, cz_s, cz_r, cp_s, cp_r, cx_s, cx_r, keep_s,
     p_s, p_r, tt_s, tt_r, col_s, col_r, row_s, row_r, blk_s, blk_r,
 ):
@@ -365,11 +416,6 @@
     def is_me(to):
         return (to[0] == e) & (to[1] == p)
 
-    def greet(who):
-        @pl.when(jnp.logical_not(is_me(who)))
-        def _():
-            pl.semaphore_signal(barrier, inc=1, device_id=who, device_id_type=MESH)
-
     def send(src, dst, send_sem, recv_sem, to, also=None):
         here, there = is_me(to), jnp.logical_not(is_me(to))
         if also is not None:
@@ -393,13 +439,6 @@
     z_row, z_col = e % 8, z
     apart = (z_col + 8 - z_row) % 8
     straight = apart <= 4
-    gap = jnp.where(straight, apart, 8 - apart)
-    z_first = jnp.where(straight, z_row, z_col)
-    h_first = jnp.where(straight, e // 8, h)
-    h_second = jnp.where(straight, h, e // 8)
-    z_from = (z_first + 8 - jnp.where(gap == 3, 1, 0)) % 8
-    c_from = jnp.where(gap == 0, h_second, jnp.where(gap >= 3, 1, 0))
-
     owners = []
     for k in range(5):
         first = (k + 1) // 2
@@ -418,28 +457,15 @@
         pl.semaphore_signal(barrier, inc=1, device_id=in_plane(q), device_id_type=MESH)
     for q in range(1, 8):
         pl.semaphore_signal(barrier, inc=1, device_id=along_z(q), device_id_type=MESH)
-    for q in range(16):
-        greet(device(q // 4, q % 4, z, h))
-        greet((q, p))
-        greet((q, e))
-    for t in range(8):
-        q = 8 * h_first + t
-        greet(device(q // 4, q % 4, z_from, c_from))
-    targets = [(q, 8 * c + z) for q in range(16)] + [(p, q) for q in range(16)] + [(q, p) for q in range(16)]
-    expected = 24
-    for to in targets:
-        expected = expected + jnp.where(is_me(to), 0, 1)
-    for _, _, to, also in owners:
-        counts = jnp.logical_not(is_me(to)) if also is None else jnp.logical_not(is_me(to)) & also
-        expected = expected + jnp.where(counts, 1, 0)
-    pl.semaphore_wait(barrier, expected)
+    points[...] = jnp.transpose(points_t[...])
+    pl.semaphore_wait(barrier, 24)
 
     drain = gather(
-        spots, desc, points, weight, half, other_weight, line, table, feats,
-        half_s, half_r, swap_s, swap_r, local_s, zp_s, zp_r, zt_s, zt_r, slab_s, slab_r, slabx_s, slabx_r,
+        spots, desc, points, weight, half, other_weight, line, table, extra, feats, feats_hi, feats_lo, rows_hi, rows_lo,
+        half_s, half_r, swap_s, swap_r, zp_s, zp_r, zt_s, zt_r, slab_s, slab_r, slabx_s, slabx_r,
         ring_s, ring_r, ringx_s, ringx_r,
     )
-    kernel_values(spots, table, feats, feats_hi, feats_lo, rows_hi, rows_lo, kp, kt)
+    drain_values = kernel_values(spots, feats_hi, feats_lo, rows_hi, rows_lo, kp, kt, kp_s, kp_r, kt_s, kt_r)
     pending, plain = [], []
 
     def go(copy):
@@ -456,11 +482,7 @@
             there = index_at(q)
             go(remote(cc.at[there % 4, corner_rows(there)], c_in.at[me], c_s.at[q], c_r.at[q], in_plane(q)))
 
-    def send_panel():
-        for q in range(16):
-            pending.append(send(pp.at[q], p_in.at[me], p_s.at[q], p_r.at[me], (q, 8 * c + z)))
-
-    multiply(spots, weight, other_weight, kp, kt, tt, pp, cc, send_corner, send_panel)
+    multiply(spots, weight, other_weight, kp, kt, tt, pp, cc, send_corner)
 
     for q in range(16):
         arrived(c_in.at[index_from(q)], c_r.at[q])
@@ -472,6 +494,9 @@
     c_z[z] = total + jnp.where(at_row == at_col, 1.0, 0.0)
     for q in range(1, 8):
         go(remote(c_z.at[z], c_z.at[z], cz_s.at[q], cz_r.at[q], along_z(q)))
+    pending.append(send(pp.at[e], p_in.at[me], p_s.at[0], p_r.at[me], (e, 8 * c + z)))
+    for q in range(1, 16):
+        go(remote(pp.at[(e + q) % 16], p_in.at[me], p_s.at[q], p_r.at[me], ((e + q) % 16, 8 * c + z)))
     for q in range(1, 8):
         arrived(c_z.at[(z + 8 - q) % 8], cz_r.at[q])
 
@@ -484,23 +509,26 @@
     keep = pltpu.make_async_copy(c_z, corner_part(me, c), keep_s)
     keep.start()
 
-    for q in range(16):
-        arrived(p_in.at[q], p_r.at[q])
-    total = p_in[0]
-    for q in range(1, 16):
-        total = total + p_in[q]
-    t_own[...] = total
-    for q in range(16):
-        pending.append(send(t_own, p_rows.at[e], row_s.at[q], row_r.at[e], (p, q)))
-        pending.append(send(t_own, p_cols.at[e], col_s.at[q], col_r.at[e], (q, p)))
-
     for q in range(1, 16):
         part = corner_part(index_from(q), c)
         arrived(part, cp_r.at[q])
         go(remote(part, part, cx_s.at[q], cx_r.at[q], sibling))
     for q in range(16):
-        go_to = device(q // 4, q % 4, z, c)
-        pending.append(send(tt.at[:, 16 * q : 16 * q + 16], tt_in.at[me], tt_s.at[q], tt_r.at[me], go_to))
+        arrived(p_in.at[q], p_r.at[q])
+    total = p_in[0]
+    for q in range(1, 16):
+        total = total + p_in[q]
+    t_own[...] = total
+    pending.append(send(t_own, p_rows.at[e], row_s.at[0], row_r.at[e], (p, p)))
+    pending.append(send(t_own, p_cols.at[e], col_s.at[0], col_r.at[e], (e, p)))
+    for q in range(1, 16):
+        go(remote(t_own, p_rows.at[e], row_s.at[q], row_r.at[e], (p, (p + q) % 16)))
+        go(remote(t_own, p_cols.at[e], col_s.at[q], col_r.at[e], ((e + q) % 16, p)))
+    stay_tt = pltpu.make_async_copy(tt.at[:, pl.ds(pl.multiple_of(16 * me, 16), 16)], tt_in.at[me], tt_r.at[me])
+    stay_tt.start()
+    for q in range(1, 16):
+        rows = pl.ds(pl.multiple_of(16 * index_at(q), 16), 16)
+        go(remote(tt.at[:, rows], tt_in.at[me], tt_s.at[q], tt_r.at[me], in_plane(q)))
     keep.wait()
     for q in range(16):
         arrived(corner_part(index_from(q), 1 - c), cx_r.at[q])
@@ -508,16 +536,27 @@
     n = a.shape[0]
     a[...] = c_all[...].reshape(n, n)
     ui[:, 128:256] = a[:, pl.ds(pl.multiple_of(128 * (e // 4), 128), 128)]
+    def apply(k):
+        lo, hi = k * NB, (k + 1) * NB
+        inv = inv_ref[k]
+        ui[lo:hi, :] = dot_hi(inv, ui[lo:hi, :], ((1,), (0,)))
+        uj[lo:hi, :] = dot_hi(inv, uj[lo:hi, :], ((1,), (0,)))
+        if hi < n:
+            u = a[lo:hi, hi:]
+            ui[hi:, :] -= dot_hi(u, ui[lo:hi, :], ((0,), (0,)))
+            uj[hi:, :] -= dot_hi(u, uj[lo:hi, :], ((0,), (0,)))
+
     for k in range(n // NB):
         lo, hi = k * NB, (k + 1) * NB
         d[...] = a[lo:hi, lo:hi]
-        inverse_factor(d, inv_ref)
-        inv = inv_ref[...]
+        inverse_factor(d, inv_ref.at[k])
+        if k >= 2:
+            apply(k - 1)
         if hi < n:
-            a[lo:hi, hi:] = dot_hi(inv, a[lo:hi, hi:], ((1,), (0,)))
+            a[lo:hi, hi:] = dot_hi(inv_ref[k], a[lo:hi, hi:], ((1,), (0,)))
             u = a[lo:hi, hi:]
             a[hi:, hi:] -= dot_hi(u, u, ((0,), (0,)))
-        if k == 0:
+        if k == 1:
             for q in range(16):
                 arrived(tt_in.at[q], tt_r.at[q])
             total = tt_in[0]
@@ -533,11 +572,8 @@
                 arrived(p_cols.at[q], col_r.at[q])
             ui[:, 0:128] = p_rows[...].reshape(n, 128)
             uj[...] = p_cols[...].reshape(n, 128)
-        ui[lo:hi, :] = dot_hi(inv, ui[lo:hi, :], ((1,), (0,)))
-        uj[lo:hi, :] = dot_hi(inv, uj[lo:hi, :], ((1,), (0,)))
-        if hi < n:
-            ui[hi:, :] -= dot_hi(u, ui[lo:hi, :], ((0,), (0,)))
-            uj[hi:, :] -= dot_hi(u, uj[lo:hi, :], ((0,), (0,)))
+            apply(0)
+    apply(n // NB - 1)
     for t in range(8):
         arrived(block.at[16 * t : 16 * t + 16], blk_r.at[t])
     gram = block[...]
@@ -545,49 +581,53 @@
     same = lax.broadcasted_iota(jnp.int32, (128, 128), 0) == lax.broadcasted_iota(jnp.int32, (128, 128), 1)
     gram = gram + jnp.where(same & (e == p), 1.0, 0.0)
     trail_ref[...] = gram - dot_hi(ui[:, 0:128], uj[...], ((0,), (0,)))
-    across = jnp.transpose(ui[pl.ds(pl.multiple_of(32 * p, 32), 32), :])
-    strip[...] = across[128:256]
-    panel_ref[0:32, :] = strip[pl.ds(pl.multiple_of(32 * (e % 4), 32), 32), :]
-    panel_ref[32:160, :] = across[0:128]
+    own_rows = ui[pl.ds(pl.multiple_of(32 * p, 32), 32), :]
+    lead = pltpu.roll(own_rows[:, 128:256], (128 - 32 * (e % 4)) % 128, 1)
+    rest = pltpu.roll(own_rows[:, 0:128], 32, 1)
+    lanes = lax.broadcasted_iota(jnp.int32, (32, 128), 1)
+    panel_ref[:, 0:128] = jnp.where(lanes < 32, lead, rest)
+    panel_ref[:, 128:160] = rest[:, 0:32]
     for copy in plain:
         copy.wait_send()
     for finish in pending:
         finish()
     drain()
-
-
-def fit(desc, points, weight):
+    drain_values()
+
+
+def fit(desc, points_t, weight):
     dma = pltpu.SemaphoreType.DMA
     vmem = pl.BlockSpec(memory_space=pltpu.VMEM)
     f32 = lambda *shape: pltpu.VMEM(shape, F32)
     bf16 = lambda *shape: pltpu.VMEM(shape, BF16)
     return pl.pallas_call(
         whole,
-        out_shape=(jax.ShapeDtypeStruct((160, 32), F32), jax.ShapeDtypeStruct((128, 128), F32)),
+        out_shape=(jax.ShapeDtypeStruct((32, 160), F32), jax.ShapeDtypeStruct((128, 128), F32)),
         in_specs=[vmem] * 3,
         out_specs=[vmem] * 2,
         scratch_shapes=[
-            f32(80, 64), f32(8, 1024), f32(384, 128), f32(2, 2, 384, 1024), f32(16, 64, 1024),
-            bf16(1024, 1024), bf16(1024, 1024), bf16(320, 1024), bf16(320, 1024),
-            f32(512, 1024), f32(3, 256, 1024), f32(5, 256, 128), f32(16, 32, 128), f32(4, 32, 128),
+            f32(160, 64), f32(80, 64), f32(1, 1024), f32(384, 128), f32(2, 384, 1024), f32(2, 64, 1024), f32(16, 64, 1024),
+            bf16(1024, 1024), bf16(1024, 1024), bf16(768, 1024), bf16(768, 1024),
+            f32(2, 8, 2, 16, 1024), f32(3, 2, 2, 64, 1024), f32(5, 256, 128), f32(16, 32, 128), f32(4, 32, 128),
             f32(16, 8, 128), f32(8, 8, 128), f32(2, 8, 4, 8, 512), f32(16, 32, 128), f32(16, 32, 128), f32(16, 32, 128),
             f32(32, 128), f32(16, 5, 16, 128), f32(5, 16, 128), f32(128, 128),
-            f32(512, 512), f32(512, 256), f32(512, 128), f32(NB, NB), f32(NB, NB), f32(128, 32),
-            dma((3,)), dma((3,)), dma((2,)), dma((2,)), dma,
+            f32(512, 512), f32(512, 256), f32(512, 128), f32(NB, NB), f32(4, NB, NB),
+            dma((3,)), dma((3,)), dma((2,)), dma((2,)),
             dma((8,)), dma((8,)), dma((4,)), dma((4,)),
             dma((16,)), dma((16,)), dma((16,)), dma((16,)),
             dma((16,)), dma((16,)), dma((16,)), dma((16,)),
+            dma((4,)), dma((4,)), dma((4,)), dma((4,)),
         ]
         + [dma((16,))] * 8
         + [dma]
         + [dma((16,))] * 10,
         compiler_params=pltpu.CompilerParams(collective_id=0, has_side_effects=True, vmem_limit_bytes=60 * 2**20),
-    )(desc, points, weight)
+    )(desc, points_t, weight)
 
 
 def local(descriptors, env_weight, points):
-    weight = jnp.broadcast_to(env_weight[None, :], (8, env_weight.shape[0]))
-    return fit(descriptors, points, weight)
+    panel_t, trailing = fit(descriptors, points.T, env_weight.reshape(1, -1))
+    return panel_t.T, trailing
 
 
 def solution(mesh):

time: 122 us -> 110 us (0.902); the launches traced: 121 us -> 110 us
  Pallas kernels: 115 us -> 108 us
  local copies, waits for them, and re-layouts: 5.1 us -> 2.04 us
    pallas_call x1, Pallas kernels: 115 us -> 108 us  [fit(): pl.pallas_call(whole, out_shape=(jax.ShapeDtypeStruct((32, 160), F32), ja...]
    pallas_call x1 -> x0, local copies, waits for them, and re-layouts: 1.61 us -> none  [fit(): pl.pallas_call(whole, out_shape=(jax.ShapeDtypeStruct((160, 32), F32), ja...]
    broadcast_in_dim x1 -> x0, local copies, waits for them, and re-layouts: 1.3 us -> none  [local(): weight = jnp.broadcast_to(env_weight[None, :], (8, env_weight.shape[0]))]
where the time goes in v5:
time: 110 us
  Pallas kernels  108 us (98%)
  local copies, waits for them, and re-layouts  2.04 us (2%)
    pallas_call x1, Pallas kernels, fit(): pl.pallas_call(whole, out_shape=(jax.ShapeDtypeStruct((32, 160), F32), ja...  108 us

profile of v5, /device:TPU:1, one launch (start us, length us, event | category | flops | bytes accessed | tf_op | source)
XLA Modules:
  0.0 110.3 jit_solution(4791686529526171336)
XLA Ops:
  0.6 107.6 %shard_map.50 = (f32[32,160]{1,0:T(8,128)}, f32[128,128]{1,0:T(8,128)}) custom-call(f32[64,1024]{1,0:T(8,128)} %desc.1, f32[64,160]{1,0:T(8,128)} %bitcast.3, f32[1,1024]{1,0:T(1,128)} %bitcast.5), custom_call_target="tpu_custom_call" | custom-call | tf_op jit(solution)/shard_map/pallas_call | solution.py:603
  108.3 0.0 copy-start
  108.3 1.4 %copy.7 = f32[160,32]{0,1:T(8,128)} copy(f32[160,32]{0,1:T(8,128)} %bitcast.4) | data formatting | bytes 40960
  109.7 0.0 copy-done
  109.7 0.6 copy.8
Async XLA Ops:
  108.3 1.4 %copy-start = (f32[128,128]{1,0:T(8,128)S(1)}, f32[128,128]{1,0:T(8,128)}, u32[]{:S(2)}) copy-start(f32[128,128]{1,0:T(8,128)} %get-tuple-element.9) | copy-start | bytes 196612

commit v6 on v5

--- a/solution.py
+++ b/solution.py
@@ -145,13 +145,6 @@
         across.append(remote(src, src, ringx_s.at[at], ringx_r.at[at], sibling))
         across[-1].start()
 
-    @pl.when(jnp.logical_not(native))
-    def _():
-        for n in range(2):
-            arrived(piece(0, n, c, turn), swap_r.at[n])
-            for copy in first[n]:
-                copy.start()
-
     for s in (1, 2, 3):
         arrived(line.at[pl.ds(128 + 64 * s, 64)], zt_r.at[s])
     for d in range(1, 8):
@@ -195,6 +188,13 @@
     forward(line, own, 0, 1, step(0, 1))
     forward(line, own, 0, 3, step(0, 3))
     to_other_core(0, line.at[third(o)], (mine_h, mine_lanes))
+    @pl.when(jnp.logical_not(native))
+    def _():
+        for n in range(2):
+            arrived(piece(0, n, c, turn), swap_r.at[n])
+            for copy in first[n]:
+                copy.start()
+
     split(line[0:256], pl.ds(pl.multiple_of(256 * mine_h, 256), 256), mine_lanes)
     split_third(line[third(c)], mine_h, c, mine_lanes)
 
@@ -348,7 +348,7 @@
 
 
 def dot_hi(a, b, dims):
-    return lax.dot_general(a, b, (dims, ((), ())), precision=HI, preferred_element_type=F32)
+    return dot3(halves(a), halves(b), dims)
 
 
 def inverse_factor(d_ref, e_ref):
@@ -373,8 +373,10 @@
             e_row.append(full(e[i : i + 1]))
             c_row.append([full(c[k][i : i + 1]) if k > i else None for k in range(8)])
             if i < 7:
-                m = jnp.where(rows > i, c[i] * r, 0.0)
-                for k in range(i + 1, 8):
+                low = jnp.where(rows > i, c[i], 0.0)
+                m = low * r
+                c[i + 1] = c[i + 1] - (low * c_row[i][i + 1]) * r
+                for k in range(i + 2, 8):
                     c[k] = c[k] - m * c_row[i][k]
                 v = v - m * v_row[i]
                 e = e - m * e_row[i]
@@ -503,15 +505,29 @@
     def corner_part(q, core):
         return c_all.at[core, :, q // 4, :, pl.ds(pl.multiple_of(128 * (q % 4), 128), 128)]
 
-    for q in range(1, 16):
-        go(remote(c_z, corner_part(me, c), cp_s.at[q], cp_r.at[q], in_plane(q)))
+    def near(j1, j2):
+        return (x + j1 * (1 - c) + j2 * c) % 4, (y + j1 * c + j2 * (1 - c)) % 4
+
+    def origin(j1, j2, core):
+        sx = (x + 8 - j1 * (1 - core) - j2 * core) % 4
+        sy = (y + 8 - j1 * core - j2 * (1 - core)) % 4
+        return 4 * sx + sy
+
+    for j in (1, 3, 2):
+        go(remote(c_z, corner_part(me, c), cp_s.at[4 * j], cp_r.at[4 * j], device(*near(j, 0), z, c)))
+    for j in (1, 3, 2):
+        go(remote(c_z, corner_part(me, c), cp_s.at[j], cp_r.at[j], device(*near(0, j), z, c)))
     go(remote(c_z, corner_part(me, c), cx_s.at[0], cx_r.at[0], sibling))
     keep = pltpu.make_async_copy(c_z, corner_part(me, c), keep_s)
     keep.start()
 
-    for q in range(1, 16):
-        part = corner_part(index_from(q), c)
+    for j1, j2 in [(j, 0) for j in (1, 3, 2)] + [(0, j) for j in (1, 3, 2)] + [(k, j) for k in (1, 3, 2) for j in (1, 3, 2)]:
+        q = 4 * j1 + j2
+        part = corner_part(origin(j1, j2, c), c)
         arrived(part, cp_r.at[q])
+        if j2 == 0:
+            for j in (1, 3, 2):
+                go(remote(part, part, cp_s.at[q + j], cp_r.at[q + j], device(*near(0, j), z, c)))
         go(remote(part, part, cx_s.at[q], cx_r.at[q], sibling))
     for q in range(16):
         arrived(p_in.at[q], p_r.at[q])
@@ -531,7 +547,7 @@
         go(remote(tt.at[:, rows], tt_in.at[me], tt_s.at[q], tt_r.at[me], in_plane(q)))
     keep.wait()
     for q in range(16):
-        arrived(corner_part(index_from(q), 1 - c), cx_r.at[q])
+        arrived(corner_part(origin(q // 4, q % 4, 1 - c), 1 - c), cx_r.at[q])
 
     n = a.shape[0]
     a[...] = c_all[...].reshape(n, n)

time: 110 us -> 119 us (1.082)
  the two profiles are of different devices: /device:TPU:1 before, /device:TPU:7 now
where the time goes in v6:
time: 119 us
  Pallas kernels  116 us (97%)
  local copies, waits for them, and re-layouts  2.04 us (2%)
    pallas_call x1, Pallas kernels, fit(): pl.pallas_call(whole, out_shape=(jax.ShapeDtypeStruct((32, 160), F32), ja...  116 us

profile of v6, /device:TPU:7, one launch (start us, length us, event | category | flops | bytes accessed | tf_op | source)
XLA Modules:
  0.0 118.8 jit_solution(11118519098416836791)
XLA Ops:
  0.6 116.1 %shard_map.50 = (f32[32,160]{1,0:T(8,128)}, f32[128,128]{1,0:T(8,128)}) custom-call(f32[64,1024]{1,0:T(8,128)} %desc.1, f32[64,160]{1,0:T(8,128)} %bitcast.3, f32[1,1024]{1,0:T(1,128)} %bitcast.5), custom_call_target="tpu_custom_call" | custom-call | tf_op jit(solution)/shard_map/pallas_call | solution.py:619
  116.7 0.0 copy-start
  116.8 1.4 %copy.7 = f32[160,32]{0,1:T(8,128)} copy(f32[160,32]{0,1:T(8,128)} %bitcast.4) | data formatting | bytes 40960
  118.2 0.0 copy-done
  118.2 0.6 copy.8
Async XLA Ops:
  116.7 1.4 %copy-start = (f32[128,128]{1,0:T(8,128)S(1)}, f32[128,128]{1,0:T(8,128)}, u32[]{:S(2)}) copy-start(f32[128,128]{1,0:T(8,128)} %get-tuple-element.9) | copy-start | bytes 196612

commit v7 on v5

--- a/solution.py
+++ b/solution.py
@@ -348,7 +348,7 @@
 
 
 def dot_hi(a, b, dims):
-    return lax.dot_general(a, b, (dims, ((), ())), precision=HI, preferred_element_type=F32)
+    return dot3(halves(a), halves(b), dims)
 
 
 def inverse_factor(d_ref, e_ref):
@@ -373,8 +373,10 @@
             e_row.append(full(e[i : i + 1]))
             c_row.append([full(c[k][i : i + 1]) if k > i else None for k in range(8)])
             if i < 7:
-                m = jnp.where(rows > i, c[i] * r, 0.0)
-                for k in range(i + 1, 8):
+                low = jnp.where(rows > i, c[i], 0.0)
+                m = low * r
+                c[i + 1] = c[i + 1] - (low * c_row[i][i + 1]) * r
+                for k in range(i + 2, 8):
                     c[k] = c[k] - m * c_row[i][k]
                 v = v - m * v_row[i]
                 e = e - m * e_row[i]

time: 110 us -> 110 us (level)
  no operation moved by 1% of the time
where the time goes in v7:
time: 110 us; the launch traced here: 109 us
  Pallas kernels  107 us (97%)
  local copies, waits for them, and re-layouts  2.04 us (2%)
    pallas_call x1, Pallas kernels, fit(): pl.pallas_call(whole, out_shape=(jax.ShapeDtypeStruct((32, 160), F32), ja...  107 us

profile of v7, /device:TPU:1, one launch (start us, length us, event | category | flops | bytes accessed | tf_op | source)
XLA Modules:
  0.0 109.4 jit_solution(14724295378738676712)
XLA Ops:
  0.6 106.7 %shard_map.50 = (f32[32,160]{1,0:T(8,128)}, f32[128,128]{1,0:T(8,128)}) custom-call(f32[64,1024]{1,0:T(8,128)} %desc.1, f32[64,160]{1,0:T(8,128)} %bitcast.3, f32[1,1024]{1,0:T(1,128)} %bitcast.5), custom_call_target="tpu_custom_call" | custom-call | tf_op jit(solution)/shard_map/pallas_call | solution.py:605
  107.4 0.0 copy-start
  107.4 1.4 %copy.7 = f32[160,32]{0,1:T(8,128)} copy(f32[160,32]{0,1:T(8,128)} %bitcast.4) | data formatting | bytes 40960
  108.8 0.0 copy-done
  108.8 0.6 copy.8
Async XLA Ops:
  107.4 1.4 %copy-start = (f32[128,128]{1,0:T(8,128)S(1)}, f32[128,128]{1,0:T(8,128)}, u32[]{:S(2)}) copy-start(f32[128,128]{1,0:T(8,128)} %get-tuple-element.9) | copy-start | bytes 196612
